TPU v7x, 32 devices: a whole 2x2x4 slice. The times are simulated.
32 devices in a mesh: wide: 8 (over z, y), narrow: 4 (over x, core).
Axes of the slice: x: 2, y: 2, z: 4, core: 2. Of those that a mesh axis runs over, the one named last changes fastest.
Arguments:
- inputs: bfloat16 [2, 1024, 16, 512], P(None, 'narrow', 'wide')
- cotangent: bfloat16 [2, 1024, 16, 512], P(None, 'narrow', 'wide'), may hold values from -6 to 6
- lengths: int32 [2, 16], P(None, 'wide'), may hold values from 102 to 1024, as said below
- ffn1_in: bfloat16 [512, 2048], P('wide', 'narrow'), may hold values from -0.25 to 0.25
- ffn1_out: bfloat16 [2048, 512], P('narrow', 'wide'), may hold values from -0.25 to 0.25
- attn_in: bfloat16 [512, 3, 512], P('wide', None, 'narrow'), may hold values from -0.25 to 0.25
- pos_proj: bfloat16 [512, 512], P('wide', 'narrow'), may hold values from -0.25 to 0.25
- attn_out: bfloat16 [512, 512], P('narrow', 'wide'), may hold values from -1.5 to 1.5
- conv_in: bfloat16 [512, 2, 512], P('wide', None, 'narrow'), may hold values from -0.25 to 0.25
- depthwise: bfloat16 [32, 512], P('wide', 'narrow'), may hold values from -1 to 1
- conv_out: bfloat16 [512, 512], P('narrow', 'wide'), may hold values from -0.375 to 0.375
- ffn2_in: bfloat16 [512, 2048], P('wide', 'narrow'), may hold values from -0.25 to 0.25
- ffn2_out: bfloat16 [2048, 512], P('narrow', 'wide'), may hold values from -0.25 to 0.25
- row_gains: bfloat16 [5, 512], replicated, may hold values from 0.099609375 to 1.8984375
- row_biases: bfloat16 [9, 512], replicated, may hold values from -2 to 2
- unit_biases: bfloat16 [5, 512], P(None, 'narrow'), may hold values from -3 to 3
- ffn_biases: bfloat16 [2, 2048], P(None, 'narrow'), may hold values from -3 to 3
- norm_affine: bfloat16 [2, 512], P(None, 'narrow'), may hold values from 0.099609375 to 1.8984375
Outputs:
- layer_out: bfloat16 [2, 1024, 16, 512], P(None, 'narrow', 'wide')
- input_grad: float32 [2, 1024, 16, 512], P(None, 'narrow', 'wide')
- grad_ffn1_in: float32 [512, 2048], P('wide', 'narrow')
- grad_ffn1_out: float32 [2048, 512], P('narrow', 'wide')
- grad_attn_in: float32 [512, 3, 512], P('wide', None, 'narrow')
- grad_pos_proj: float32 [512, 512], P('wide', 'narrow')
- grad_attn_out: float32 [512, 512], P('narrow', 'wide')
- grad_conv_in: float32 [512, 2, 512], P('wide', None, 'narrow')
- grad_depthwise: float32 [32, 512], P('wide', 'narrow')
- grad_conv_out: float32 [512, 512], P('narrow', 'wide')
- grad_ffn2_in: float32 [512, 2048], P('wide', 'narrow')
- grad_ffn2_out: float32 [2048, 512], P('narrow', 'wide')
- grad_row_gains: float32 [5, 512], replicated
- grad_row_biases: float32 [9, 512], replicated
- grad_unit_biases: float32 [5, 512], P(None, 'narrow')
- grad_ffn_biases: float32 [2, 2048], P(None, 'narrow')
- grad_norm_affine: float32 [2, 512], P(None, 'narrow')
Inputs may be any that keep to these rules, and one draw needn't show every extreme that they name: `lengths`: in each micro-batch one utterance has 1024 frames and another has the fewest frames allowed.
All inputs are finite; a program needn't handle non-finite values.
Results may differ from a plain program's by a relative error of at most 0.03.
Values may be sent and summed in bfloat16 or wider, within the bound.
No kernel may reach another device: no remote copies, remote signals or barrier semaphores. Data moves between devices by JAX's collectives and lax.ppermute only.
A program may use at most 320 MiB of HBM per device.

v0:
```python
from functools import partial
import math

import jax
import jax.numpy as jnp
from jax import lax
from jax.sharding import PartitionSpec as P

FF = 2048
HEAD_DIM = 64
LMAX = 1024
QBLOCK = 512


EPSILON = 1e-05
MASKED = -1e30


def norm_rows(stream, scale_row, shift_row):
    center = stream - jnp.mean(stream, axis=-1, keepdims=True)
    inverse = lax.rsqrt(jnp.mean(center * center, axis=-1, keepdims=True) + EPSILON)
    normal = center * inverse
    return (normal * scale_row + shift_row, normal, inverse)


def norm_rows_back(upstream, normal, inverse, scale_row):
    scaled = upstream * scale_row
    mean_plain = jnp.mean(scaled, axis=-1, keepdims=True)
    mean_cross = jnp.mean(scaled * normal, axis=-1, keepdims=True)
    grad_rows = inverse * (scaled - mean_plain - normal * mean_cross)
    return (grad_rows, jnp.sum(upstream * normal, axis=(0, 1)), jnp.sum(upstream, axis=(0, 1)))


def silu_slope(values_in):
    sigma = jax.nn.sigmoid(values_in)
    return sigma * (1.0 + values_in * (1.0 - sigma))


def position_table(length, feature_count):
    offsets = (length - 1 - jnp.arange(2 * length - 1)).astype(jnp.float32)
    freq_index = jnp.arange(feature_count // 2).astype(jnp.float32)
    frequency = jnp.exp(freq_index * (-2.0 * math.log(10000.0) / feature_count))
    angles = offsets[:, None] * frequency[None, :]
    return jnp.stack([jnp.sin(angles), jnp.cos(angles)], axis=-1).reshape(
        2 * length - 1, feature_count
    )


def shift_rows(raw_scores, block_rows, key_count):
    padded = jnp.pad(raw_scores, ((0, 0), (0, 1)))
    flattened = padded.reshape(-1)
    flattened = lax.slice_in_dim(
        flattened, block_rows - 1, block_rows - 1 + block_rows * (block_rows + key_count - 1)
    )
    return flattened.reshape(block_rows, block_rows + key_count - 1)[:, :key_count]


def unshift_rows(grad_scores, block_rows, key_count):
    padded = jnp.pad(grad_scores, ((0, 0), (0, block_rows - 1)))
    flattened = jnp.pad(padded.reshape(-1), (block_rows - 1, 1))
    return flattened.reshape(block_rows, block_rows + key_count)[:, : block_rows + key_count - 1]


def to_heads(values_in):
    return values_in.reshape(values_in.shape[0], values_in.shape[1], -1, HEAD_DIM)


def spread_rows(values_in):
    return lax.all_gather(values_in, "narrow", axis=0, tiled=True)


def fold_rows(partial_sums):
    return lax.psum_scatter(partial_sums, "narrow", scatter_dimension=0, tiled=True)


def spread_grads(values_in):
    return lax.all_gather(values_in, "narrow", axis=0, tiled=True)


def fold_grads(partial_sums):
    return lax.psum_scatter(partial_sums, "narrow", scatter_dimension=0, tiled=True)


def place_columns(values_in, feature_count, narrow_index):
    width = values_in.shape[1]
    zero_index = jnp.zeros((), jnp.int32)
    return lax.dynamic_update_slice(
        jnp.zeros((values_in.shape[0], feature_count), jnp.float32),
        values_in,
        (zero_index, narrow_index * width),
    )


def block_scores(rows_c, rows_p, key_head, window, valid_keys, scale):
    key_count = key_head.shape[0]
    block_rows = rows_c.shape[0]
    content = jnp.einsum("qd,kd->qk", rows_c, key_head, preferred_element_type=jnp.float32)
    raw_scores = jnp.einsum("qd,wd->qw", rows_p, window, preferred_element_type=jnp.float32)
    scores = (content + shift_rows(raw_scores, block_rows, key_count)) * scale
    return jnp.where(valid_keys[None, :], scores, MASKED)


def head_forward(query_c, query_p, key_head, value_head, pos_head, valid_keys, block_rows, scale):
    length = key_head.shape[0]
    contexts = []
    totals = []
    for row_begin in range(0, length, block_rows):
        row_end = row_begin + block_rows
        window = pos_head[length - row_end : 2 * length - 1 - row_begin]
        scores = block_scores(
            query_c[row_begin:row_end],
            query_p[row_begin:row_end],
            key_head,
            window,
            valid_keys,
            scale,
        )
        row_max = jnp.max(scores, axis=1, keepdims=True)
        row_total = jnp.sum(jnp.exp(scores - row_max), axis=1, keepdims=True)
        log_total = row_max + jnp.log(row_total)
        probabilities = jnp.exp(scores - log_total).astype(jnp.bfloat16)
        contexts.append(jnp.dot(probabilities, value_head, preferred_element_type=jnp.float32))
        totals.append(log_total[:, 0])
    return (jnp.concatenate(contexts, 0), jnp.concatenate(totals, 0))


def head_backward(
    query_c,
    query_p,
    key_head,
    value_head,
    pos_head,
    valid_keys,
    log_total,
    grad_context,
    block_rows,
    scale,
):
    length = key_head.shape[0]
    grads_c = []
    grads_p = []
    grad_key = jnp.zeros(key_head.shape, jnp.float32)
    grad_value = jnp.zeros(value_head.shape, jnp.float32)
    grad_pos = jnp.zeros(pos_head.shape, jnp.float32)
    for row_begin in range(0, length, block_rows):
        row_end = row_begin + block_rows
        pos_lower = length - row_end
        window = pos_head[pos_lower : 2 * length - 1 - row_begin]
        rows_c = query_c[row_begin:row_end]
        rows_p = query_p[row_begin:row_end]
        scores = block_scores(rows_c, rows_p, key_head, window, valid_keys, scale)
        probabilities = jnp.exp(scores - log_total[row_begin:row_end, None])
        rows_grad = grad_context[row_begin:row_end]
        grad_probs = jnp.einsum(
            "qd,kd->qk", rows_grad, value_head, preferred_element_type=jnp.float32
        )
        center = jnp.sum(probabilities * grad_probs, axis=1, keepdims=True)
        grad_scores = (probabilities * (grad_probs - center)).astype(jnp.bfloat16)
        grads_c.append(
            jnp.einsum("qk,kd->qd", grad_scores, key_head, preferred_element_type=jnp.float32)
            * scale
        )
        grad_key = (
            grad_key
            + jnp.einsum("qk,qd->kd", grad_scores, rows_c, preferred_element_type=jnp.float32)
            * scale
        )
        grad_value = grad_value + jnp.einsum(
            "qk,qd->kd",
            probabilities.astype(jnp.bfloat16),
            rows_grad,
            preferred_element_type=jnp.float32,
        )
        grad_raw = unshift_rows(grad_scores, block_rows, length)
        grads_p.append(
            jnp.einsum("qw,wd->qd", grad_raw, window, preferred_element_type=jnp.float32) * scale
        )
        pos_term = (
            jnp.einsum("qw,qd->wd", grad_raw, rows_p, preferred_element_type=jnp.float32) * scale
        )
        grad_pos = grad_pos + jnp.pad(pos_term, ((pos_lower, row_begin), (0, 0)))
    return (
        jnp.concatenate(grads_c, 0),
        jnp.concatenate(grads_p, 0),
        grad_key,
        grad_value,
        grad_pos,
    )


def ffn_forward(stream, scale_row, shift_row, w_in, hidden_bias, w_out):
    normed, normal, inverse = norm_rows(stream, scale_row, shift_row)
    normed = normed.astype(jnp.bfloat16)
    source = spread_rows(normed)
    pre_act = jnp.einsum(
        "lud,df->luf", source, w_in, preferred_element_type=jnp.float32
    ) + hidden_bias.astype(jnp.float32)
    activated = jax.nn.silu(pre_act).astype(jnp.bfloat16)
    partial_sums = jnp.einsum("luf,fd->lud", activated, w_out, preferred_element_type=jnp.float32)
    partial_sums = fold_rows(partial_sums)
    return (partial_sums, (source, pre_act, activated, normal, inverse))


def ffn_backward(upstream, saved, scale_row, w_in, w_out, narrow_index):
    source, pre_act, activated, normal, inverse = saved
    half_grad = 0.5 * upstream
    grad_part = half_grad.astype(jnp.bfloat16)
    grad_part = spread_grads(grad_part)
    grad_act = jnp.einsum("lud,fd->luf", grad_part, w_out, preferred_element_type=jnp.float32)
    grad_wout = jnp.einsum("luf,lud->fd", activated, grad_part, preferred_element_type=jnp.float32)
    grad_pre = (grad_act * silu_slope(pre_act)).astype(jnp.bfloat16)
    grad_win = jnp.einsum("lud,luf->df", source, grad_pre, preferred_element_type=jnp.float32)
    bias_grad = jnp.sum(grad_pre.astype(jnp.float32), axis=(0, 1))
    grad_normed = jnp.einsum("luf,df->lud", grad_pre, w_in, preferred_element_type=jnp.float32)
    grad_normed = fold_grads(grad_normed)
    bias_grad = lax.dynamic_update_slice(
        jnp.zeros((FF,), jnp.float32), bias_grad, (narrow_index * bias_grad.shape[0],)
    )
    grad_rows, grad_scale, grad_shift = norm_rows_back(grad_normed, normal, inverse, scale_row)
    return (
        upstream + grad_rows,
        (grad_win, grad_wout, bias_grad, grad_scale, grad_shift, jnp.sum(half_grad, axis=(0, 1))),
    )


def attention_forward(
    stream, scale_row, shift_row, w_qkv, w_pos, w_out, unit_rows, valid_full, pos_table
):
    normed, normal, inverse = norm_rows(stream, scale_row, shift_row)
    source = spread_rows(normed.astype(jnp.bfloat16))
    length, utter_count = (source.shape[0], source.shape[1])
    project = jnp.einsum("lud,dke->luke", source, w_qkv, preferred_element_type=jnp.float32)
    value_all = (project[:, :, 2] + unit_rows[0]).astype(jnp.bfloat16)
    key_all = project[:, :, 1].astype(jnp.bfloat16)
    query_c = (project[:, :, 0] + unit_rows[1]).astype(jnp.bfloat16)
    query_p = (project[:, :, 0] + unit_rows[2]).astype(jnp.bfloat16)
    pos_all = jnp.dot(pos_table, w_pos, preferred_element_type=jnp.float32).astype(jnp.bfloat16)
    pos_heads = pos_all.reshape(pos_all.shape[0], -1, HEAD_DIM)
    step_head = partial(head_forward, block_rows=QBLOCK, scale=1.0 / math.sqrt(HEAD_DIM))
    per_head = jax.vmap(step_head, in_axes=(1, 1, 1, 1, 1, None), out_axes=1)
    per_utter = jax.vmap(per_head, in_axes=(1, 1, 1, 1, None, 1), out_axes=1)
    context, log_total = per_utter(
        to_heads(query_c),
        to_heads(query_p),
        to_heads(key_all),
        to_heads(value_all),
        pos_heads,
        valid_full,
    )
    context = context.reshape(length, utter_count, -1).astype(jnp.bfloat16)
    partial_sums = jnp.einsum("lue,ed->lud", context, w_out, preferred_element_type=jnp.float32)
    saved = (
        normal,
        inverse,
        source,
        query_c,
        query_p,
        key_all,
        value_all,
        pos_heads,
        log_total,
        context,
        valid_full,
    )
    return (fold_rows(partial_sums), saved)


def attention_backward(upstream, saved, scale_row, w_qkv, w_out, pos_table):
    (
        normal,
        inverse,
        source,
        query_c,
        query_p,
        key_all,
        value_all,
        pos_heads,
        log_total,
        context,
        valid_full,
    ) = saved
    length, utter_count = (source.shape[0], source.shape[1])
    grad_out = spread_grads(upstream.astype(jnp.bfloat16))
    grad_wout = jnp.einsum("lue,lud->ed", context, grad_out, preferred_element_type=jnp.float32)
    grad_context = jnp.einsum(
        "lud,ed->lue", grad_out, w_out, preferred_element_type=jnp.float32
    ).astype(jnp.bfloat16)
    step_head = partial(head_backward, block_rows=QBLOCK, scale=1.0 / math.sqrt(HEAD_DIM))
    per_head = jax.vmap(step_head, in_axes=(1, 1, 1, 1, 1, None, 1, 1), out_axes=(1, 1, 1, 1, 1))
    per_utter = jax.vmap(per_head, in_axes=(1, 1, 1, 1, None, 1, 1, 1), out_axes=(1, 1, 1, 1, 0))
    grad_c, grad_p, grad_key, grad_value, grad_pos = per_utter(
        to_heads(query_c),
        to_heads(query_p),
        to_heads(key_all),
        to_heads(value_all),
        pos_heads,
        valid_full,
        log_total,
        to_heads(grad_context),
    )
    grad_c = grad_c.reshape(length, utter_count, -1)
    grad_p = grad_p.reshape(length, utter_count, -1)
    grad_query = (grad_c + grad_p).astype(jnp.bfloat16)
    grad_key_low = grad_key.reshape(length, utter_count, -1).astype(jnp.bfloat16)
    grad_value_low = grad_value.reshape(length, utter_count, -1).astype(jnp.bfloat16)
    unit_grads = jnp.stack(
        [
            jnp.sum(grad_value_low.astype(jnp.float32), axis=(0, 1)),
            jnp.sum(grad_c, axis=(0, 1)),
            jnp.sum(grad_p, axis=(0, 1)),
        ]
    )
    grad_project = jnp.stack([grad_query, grad_key_low, grad_value_low], axis=2)
    grad_wqkv = jnp.einsum(
        "lud,luke->dke", source, grad_project, preferred_element_type=jnp.float32
    )
    grad_pos_all = jnp.sum(grad_pos, axis=0).reshape(pos_heads.shape[0], -1).astype(jnp.bfloat16)
    grad_wpos = jnp.einsum("pd,pe->de", pos_table, grad_pos_all, preferred_element_type=jnp.float32)
    grad_normed = fold_grads(
        jnp.einsum("luke,dke->lud", grad_project, w_qkv, preferred_element_type=jnp.float32)
    )
    grad_rows, grad_scale, grad_shift = norm_rows_back(grad_normed, normal, inverse, scale_row)
    return (
        upstream + grad_rows,
        (
            grad_wqkv,
            grad_wpos,
            grad_wout,
            unit_grads,
            grad_scale,
            grad_shift,
            jnp.sum(upstream, axis=(0, 1)),
        ),
    )


def conv_forward(stream, scale_row, shift_row, conv_set, mask_full, local_count):
    w_in, w_depth, w_out, conv_units, affine = conv_set
    normed, normal, inverse = norm_rows(stream, scale_row, shift_row)
    source = spread_rows(normed.astype(jnp.bfloat16))
    length = source.shape[0]
    pre_act = (
        jnp.einsum("lud,dke->luke", source, w_in, preferred_element_type=jnp.float32) + conv_units
    )
    sigma = jax.nn.sigmoid(pre_act[:, :, 1])
    gated = pre_act[:, :, 0] * sigma * mask_full[:, :, None]
    tap_count = w_depth.shape[0]
    padded = jnp.pad(gated, ((tap_count // 2 - 1, tap_count // 2), (0, 0), (0, 0)))
    depth_kernel = w_depth.astype(jnp.float32)
    mixed = depth_kernel[0] * padded[0:length]
    for tap_index in range(1, tap_count):
        mixed = mixed + depth_kernel[tap_index] * padded[tap_index : tap_index + length]
    masked = mixed * mask_full[:, :, None]
    channel_sum, count = lax.psum((jnp.sum(masked, axis=(0, 1)), local_count), "wide")
    center = mixed - channel_sum / count
    spread = lax.psum(jnp.sum(center * center * mask_full[:, :, None], axis=(0, 1)), "wide") / count
    inverse_bn = lax.rsqrt(spread + EPSILON)
    normal_bn = center * inverse_bn
    normed_bn = normal_bn * affine[0] + affine[1]
    activated = jax.nn.silu(normed_bn).astype(jnp.bfloat16)
    partial_sums = jnp.einsum("lue,ed->lud", activated, w_out, preferred_element_type=jnp.float32)
    saved = (
        normal,
        inverse,
        source,
        pre_act,
        sigma,
        padded,
        normal_bn,
        inverse_bn,
        normed_bn,
        activated,
        count,
        mask_full,
    )
    return (fold_rows(partial_sums), saved)


def conv_backward(upstream, saved, scale_row, conv_set, narrow_index):
    w_in, w_depth, w_out, conv_units, affine = conv_set
    (
        normal,
        inverse,
        source,
        pre_act,
        sigma,
        padded,
        normal_bn,
        inverse_bn,
        normed_bn,
        activated,
        count,
        mask_use,
    ) = saved
    length = source.shape[0]
    feature_count = upstream.shape[2]
    grad_part = upstream.astype(jnp.bfloat16)
    grad_part = spread_grads(grad_part)
    grad_wout = jnp.einsum("lue,lud->ed", activated, grad_part, preferred_element_type=jnp.float32)
    grad_act = jnp.einsum("lud,ed->lue", grad_part, w_out, preferred_element_type=jnp.float32)
    grad_bn = grad_act * silu_slope(normed_bn)
    sum_plain, sum_cross = lax.psum(
        (jnp.sum(grad_bn, axis=(0, 1)), jnp.sum(grad_bn * normal_bn, axis=(0, 1))), "wide"
    )
    grad_mixed = (
        inverse_bn
        * affine[0]
        * (grad_bn - mask_use[:, :, None] * (sum_plain + normal_bn * sum_cross) / count)
    )
    tap_count = w_depth.shape[0]
    depth_kernel = w_depth.astype(jnp.float32)
    back_pad = jnp.pad(grad_mixed, ((tap_count // 2, tap_count // 2 - 1), (0, 0), (0, 0)))
    grad_gated = depth_kernel[0] * back_pad[tap_count - 1 : tap_count - 1 + length]
    for tap_index in range(1, tap_count):
        offset_start = tap_count - 1 - tap_index
        grad_gated = (
            grad_gated + depth_kernel[tap_index] * back_pad[offset_start : offset_start + length]
        )
    grad_depth = jnp.stack(
        [
            jnp.sum(grad_mixed * padded[tap_index : tap_index + length], axis=(0, 1))
            for tap_index in range(tap_count)
        ]
    )
    grad_gated = grad_gated * mask_use[:, :, None]
    grad_value = grad_gated * sigma
    grad_gate = grad_gated * pre_act[:, :, 0] * sigma * (1.0 - sigma)
    grad_pre = jnp.stack([grad_value, grad_gate], axis=2).astype(jnp.bfloat16)
    unit_grads = jnp.sum(grad_pre.astype(jnp.float32), axis=(0, 1))
    grad_win = jnp.einsum("lud,luke->dke", source, grad_pre, preferred_element_type=jnp.float32)
    grad_normed = jnp.einsum("luke,dke->lud", grad_pre, w_in, preferred_element_type=jnp.float32)
    norm_grads = jnp.stack([sum_cross, sum_plain])
    grad_normed = fold_grads(grad_normed)
    unit_grads = place_columns(unit_grads, feature_count, narrow_index)
    grad_rows, grad_scale, grad_shift = norm_rows_back(grad_normed, normal, inverse, scale_row)
    return (
        upstream + grad_rows,
        (
            grad_win,
            grad_depth,
            grad_wout,
            unit_grads,
            norm_grads,
            grad_scale,
            grad_shift,
            jnp.sum(upstream, axis=(0, 1)),
        ),
    )


def fetch_weights(
    ffn1_in, ffn1_out, attn_in, pos_proj, attn_out, conv_in, depthwise, conv_out, ffn2_in, ffn2_out
):
    return (
        lax.all_gather(ffn1_in, "wide", axis=0, tiled=True),
        lax.all_gather(ffn1_out, "wide", axis=1, tiled=True),
        lax.all_gather(attn_in, "wide", axis=0, tiled=True),
        lax.all_gather(pos_proj, "wide", axis=0, tiled=True),
        lax.all_gather(attn_out, "wide", axis=1, tiled=True),
        lax.all_gather(conv_in, "wide", axis=0, tiled=True),
        lax.all_gather(depthwise, "wide", axis=0, tiled=True),
        lax.all_gather(conv_out, "wide", axis=1, tiled=True),
        lax.all_gather(ffn2_in, "wide", axis=0, tiled=True),
        lax.all_gather(ffn2_out, "wide", axis=1, tiled=True),
    )


def widen_ffn(gathered, ffn_biases):
    return (gathered[0], gathered[1], gathered[8], gathered[9], ffn_biases)


def widen_conv(gathered, unit_biases, norm_affine):
    return (
        gathered[5],
        gathered[6],
        gathered[7],
        unit_biases[3:5].astype(jnp.float32),
        norm_affine.astype(jnp.float32),
    )


def shards(
    inputs,
    cotangent,
    lengths,
    ffn1_in,
    ffn1_out,
    attn_in,
    pos_proj,
    attn_out,
    conv_in,
    depthwise,
    conv_out,
    ffn2_in,
    ffn2_out,
    row_gains,
    row_biases,
    unit_biases,
    ffn_biases,
    norm_affine,
):
    micro_count, local_rows = (inputs.shape[0], inputs.shape[1])
    feature_count = inputs.shape[3]
    narrow_index = lax.axis_index("narrow")
    row_start = narrow_index * local_rows
    scale_rows = row_gains.astype(jnp.float32)
    shift_rows_all = row_biases.astype(jnp.float32)
    unit_rows = unit_biases.astype(jnp.float32)
    pos_table = position_table(LMAX, feature_count).astype(jnp.bfloat16)
    outputs = []
    input_grads = []
    totals = None
    for micro_index in range(micro_count):
        front_weights = fetch_weights(
            ffn1_in,
            ffn1_out,
            attn_in,
            pos_proj,
            attn_out,
            conv_in,
            depthwise,
            conv_out,
            ffn2_in,
            ffn2_out,
        )
        front_ffn = widen_ffn(front_weights, ffn_biases)
        front_conv = widen_conv(front_weights, unit_biases, norm_affine)
        utter_lengths = lengths[micro_index]
        valid_full = jnp.arange(LMAX)[:, None] < utter_lengths[None, :]
        mask_full = valid_full.astype(jnp.float32)
        mask_local = (
            (row_start + jnp.arange(local_rows))[:, None] < utter_lengths[None, :]
        ).astype(jnp.float32)
        local_count = jnp.sum(utter_lengths).astype(jnp.float32)
        stream_zero = inputs[micro_index].astype(jnp.float32)
        ffn_first, saved_first = ffn_forward(
            stream_zero,
            scale_rows[0],
            shift_rows_all[0],
            front_ffn[0],
            front_ffn[4][0],
            front_ffn[1],
        )
        stream_one = stream_zero + 0.5 * (ffn_first + shift_rows_all[5])
        attended, saved_att = attention_forward(
            stream_one,
            scale_rows[1],
            shift_rows_all[1],
            front_weights[2],
            front_weights[3],
            front_weights[4],
            unit_rows,
            valid_full,
            pos_table,
        )
        stream_two = stream_one + attended + shift_rows_all[6]
        convolved, saved_conv = conv_forward(
            stream_two, scale_rows[2], shift_rows_all[2], front_conv, mask_full, local_count
        )
        stream_three = stream_two + convolved + shift_rows_all[7]
        ffn_second, saved_second = ffn_forward(
            stream_three,
            scale_rows[3],
            shift_rows_all[3],
            front_ffn[2],
            front_ffn[4][1],
            front_ffn[3],
        )
        stream_four = stream_three + 0.5 * (ffn_second + shift_rows_all[8])
        final_rows, normal_final, inverse_final = norm_rows(
            stream_four, scale_rows[4], shift_rows_all[4]
        )
        outputs.append(final_rows.astype(jnp.bfloat16))
        back_weights = fetch_weights(
            ffn1_in,
            ffn1_out,
            attn_in,
            pos_proj,
            attn_out,
            conv_in,
            depthwise,
            conv_out,
            ffn2_in,
            ffn2_out,
        )
        back_ffn = widen_ffn(back_weights, ffn_biases)
        back_conv = widen_conv(back_weights, unit_biases, norm_affine)
        grad_final = cotangent[micro_index].astype(jnp.float32) * mask_local[:, :, None]
        grad_four, scale_final, shift_final = norm_rows_back(
            grad_final, normal_final, inverse_final, scale_rows[4]
        )
        grad_three, second_parts = ffn_backward(
            grad_four, saved_second, scale_rows[3], back_ffn[2], back_ffn[3], narrow_index
        )
        grad_two, conv_parts = conv_backward(
            grad_three, saved_conv, scale_rows[2], back_conv, narrow_index
        )
        grad_one, att_parts = attention_backward(
            grad_two, saved_att, scale_rows[1], back_weights[2], back_weights[4], pos_table
        )
        grad_zero, first_parts = ffn_backward(
            grad_one, saved_first, scale_rows[0], back_ffn[0], back_ffn[1], narrow_index
        )
        input_grads.append(grad_zero)
        step_grads = (
            first_parts[0],
            first_parts[1],
            att_parts[0],
            att_parts[1],
            att_parts[2],
            conv_parts[0],
            conv_parts[1],
            conv_parts[2],
            second_parts[0],
            second_parts[1],
            jnp.stack([first_parts[3], att_parts[4], conv_parts[5], second_parts[3], scale_final]),
            jnp.stack(
                [
                    first_parts[4],
                    att_parts[5],
                    conv_parts[6],
                    second_parts[4],
                    shift_final,
                    first_parts[5],
                    att_parts[6],
                    conv_parts[7],
                    second_parts[5],
                ]
            ),
            jnp.concatenate(
                [place_columns(att_parts[3], feature_count, narrow_index), conv_parts[3]], axis=0
            ),
            jnp.stack([first_parts[2], second_parts[2]]),
            conv_parts[4],
        )
        if totals is None:
            totals = step_grads
        else:
            totals = jax.tree.map(jnp.add, totals, step_grads)
    local_width = unit_biases.shape[1]
    local_hidden = ffn_biases.shape[1]
    sum_gains, sum_shifts, sum_units, sum_hidden = lax.psum(
        (totals[10], totals[11], totals[12], totals[13]), ("wide", "narrow")
    )
    grad_units = lax.dynamic_slice_in_dim(sum_units, narrow_index * local_width, local_width, 1)
    grad_hidden = lax.dynamic_slice_in_dim(sum_hidden, narrow_index * local_hidden, local_hidden, 1)
    ffn_parts = (totals[0], totals[1], totals[8], totals[9])
    conv_grad_parts = (totals[5], totals[6], totals[7])
    matrix_grads = (
        lax.psum_scatter(ffn_parts[0], "wide", scatter_dimension=0, tiled=True),
        lax.psum_scatter(ffn_parts[1], "wide", scatter_dimension=1, tiled=True),
        lax.psum_scatter(totals[2], "wide", scatter_dimension=0, tiled=True),
        lax.psum_scatter(totals[3], "wide", scatter_dimension=0, tiled=True),
        lax.psum_scatter(totals[4], "wide", scatter_dimension=1, tiled=True),
        lax.psum_scatter(conv_grad_parts[0], "wide", scatter_dimension=0, tiled=True),
        lax.psum_scatter(conv_grad_parts[1], "wide", scatter_dimension=0, tiled=True),
        lax.psum_scatter(conv_grad_parts[2], "wide", scatter_dimension=1, tiled=True),
        lax.psum_scatter(ffn_parts[2], "wide", scatter_dimension=0, tiled=True),
        lax.psum_scatter(ffn_parts[3], "wide", scatter_dimension=1, tiled=True),
    )
    return (
        jnp.stack(outputs),
        jnp.stack(input_grads),
        matrix_grads[0],
        matrix_grads[1],
        matrix_grads[2],
        matrix_grads[3],
        matrix_grads[4],
        matrix_grads[5],
        matrix_grads[6],
        matrix_grads[7],
        matrix_grads[8],
        matrix_grads[9],
        sum_gains,
        sum_shifts,
        grad_units,
        grad_hidden,
        totals[14],
    )


def solution(mesh):
    placed = (
        P(None, "narrow", "wide", None),
        P(None, "narrow", "wide", None),
        P(None, "wide"),
        P("wide", "narrow"),
        P("narrow", "wide"),
        P("wide", None, "narrow"),
        P("wide", "narrow"),
        P("narrow", "wide"),
        P("wide", None, "narrow"),
        P("wide", "narrow"),
        P("narrow", "wide"),
        P("wide", "narrow"),
        P("narrow", "wide"),
        P(),
        P(),
        P(None, "narrow"),
        P(None, "narrow"),
        P(None, "narrow"),
    )
    return jax.shard_map(
        shards,
        mesh=mesh,
        in_specs=placed,
        out_specs=(
            P(None, "narrow", "wide", None),
            P(None, "narrow", "wide", None),
            P("wide", "narrow"),
            P("narrow", "wide"),
            P("wide", None, "narrow"),
            P("wide", "narrow"),
            P("narrow", "wide"),
            P("wide", None, "narrow"),
            P("wide", "narrow"),
            P("narrow", "wide"),
            P("wide", "narrow"),
            P("narrow", "wide"),
            P(),
            P(),
            P(None, "narrow"),
            P(None, "narrow"),
            P(None, "narrow"),
        ),
        check_vma=False,
    )
```

profile of v0, /device:TPU:0, one launch (start us, length us, event | category | flops | bytes accessed | tf_op | source)
XLA Modules:
  0.0 2629.7 jit_solution(1706099105640649273)
XLA Ops:
  16.0 33.1 %all_gather.53 = bf16[512,512]{1,0:T(8,128)(2,1)S(1)} all-gather(bf16[64,512]{1,0:T(8,128)(2,1)S(1)} %copy-done.158), channel_id=1, replica_groups=mesh['wide'=8,'narrow'=4] {'wide'}, dimensions={0}, use_global_device_ids=true | all-gather | bytes 589824 | tf_op jit(solution)/shard_map/all_gather | solution.py:455
  49.1 31.2 %all_gather.108 = bf16[512,512]{0,1:T(8,128)(2,1)S(1)} all-gather(bf16[512,64]{0,1:T(8,128)(2,1)S(1)} %copy-done.159), channel_id=1, replica_groups=mesh['wide'=8,'narrow'=4] {'wide'}, dimensions={1}, use_global_device_ids=true | all-gather | bytes 589824 | tf_op jit(solution)/shard_map/all_gather | solution.py:456
  97.1 37.5 %reduce-scatter.26.cloned.1.call-done = f32[256,2,512]{2,0,1:T(8,128)} async-done(((f32[1024,2,512]{2,0,1:T(8,128)}), f32[256,2,512]{2,0,1:T(8,128)}) %reduce-scatter.26.cloned.1.call-update) | async-done | bytes 1048592 | tf_op jit(solution)/shard_map/reduce_scatter | solution.py:73
  134.6 47.0 %reduce-scatter.34.cloned.1.call-done = f32[256,2,512]{2,0,1:T(8,128)} async-done(((f32[1024,2,512]{2,0,1:T(8,128)}), f32[256,2,512]{2,0,1:T(8,128)}) %reduce-scatter.34.cloned.1.call-update) | async-done | bytes 1048592 | tf_op jit(solution)/shard_map/reduce_scatter | solution.py:73
  186.8 60.4 %multiply_sine_fusion = (bf16[2047,256,1]{0,2,1:T(2,128)(2,1)S(1)}, bf16[2047,256,1]{0,2,1:T(2,128)(2,1)S(1)}) fusion(f32[2047]{0:T(1024)S(1)} %subtract_convert_fusion, f32[256]{0:T(256)S(1)} %multiply_exponential_fusion), kind=kLoop, calls=%fused_computation.101 | loop fusion | flops 1572096 | bytes 2105340 | tf_op jit(solution)/shard_map/sin | solution.py:44
  256.2 32.6 %all_gather.112 = bf16[128,512]{0,1:T(8,128)(2,1)} all-gather(bf16[128,64]{0,1:T(8,128)(2,1)S(1)} %copy-done.217), channel_id=1, replica_groups=mesh['wide'=8,'narrow'=4] {'wide'}, dimensions={1}, use_global_device_ids=true | all-gather | bytes 147456 | tf_op jit(solution)/shard_map/all_gather | solution.py:459
  288.8 30.5 %all_gather.111 = bf16[512,128]{1,0:T(8,128)(2,1)S(1)} all-gather(bf16[64,128]{1,0:T(8,128)(2,1)S(1)} %copy-done.218), channel_id=1, replica_groups=mesh['wide'=8,'narrow'=4] {'wide'}, dimensions={0}, use_global_device_ids=true | all-gather | bytes 147456 | tf_op jit(solution)/shard_map/all_gather | solution.py:458
  320.0 31.2 %all_gather.110 = bf16[512,3,128]{2,0,1:T(8,128)(2,1)S(1)} all-gather(bf16[64,3,128]{2,0,1:T(8,128)(2,1)S(1)} %copy-done.188), channel_id=1, replica_groups=mesh['wide'=8,'narrow'=4] {'wide'}, dimensions={0}, use_global_device_ids=true | all-gather | bytes 442368 | tf_op jit(solution)/shard_map/all_gather | solution.py:457
  380.6 21.7 reshape.815
  418.6 26.1 reshape.883
  469.4 21.9 reshape.813
  507.5 26.1 reshape.879
  571.7 22.2 reshape.819
  610.1 26.0 reshape.885
  652.9 21.7 reshape.817
  690.8 26.2 reshape.884
  737.8 44.8 %reduce-scatter.36.cloned.1.call-done = f32[256,2,512]{2,0,1:T(8,128)} async-done(((f32[1024,2,512]{2,0,1:T(8,128)}), f32[256,2,512]{2,0,1:T(8,128)}) %reduce-scatter.36.cloned.1.call-update) | async-done | bytes 1048592 | tf_op jit(solution)/shard_map/reduce_scatter | solution.py:73
  788.9 20.5 all-gather
  809.5 32.5 %all_gather.116 = bf16[128,512]{0,1:T(8,128)(2,1)} all-gather(bf16[128,64]{0,1:T(8,128)(2,1)S(1)} %copy-done.219), channel_id=1, replica_groups=mesh['wide'=8,'narrow'=4] {'wide'}, dimensions={1}, use_global_device_ids=true | all-gather | bytes 147456 | tf_op jit(solution)/shard_map/all_gather | solution.py:462
  842.0 30.7 %all_gather.115 = bf16[512,2,128]{2,0,1:T(8,128)(2,1)S(1)} all-gather(bf16[64,2,128]{2,0,1:T(8,128)(2,1)S(1)} %copy.179), channel_id=1, replica_groups=mesh['wide'=8,'narrow'=4] {'wide'}, dimensions={0}, use_global_device_ids=true | all-gather | bytes 294912 | tf_op jit(solution)/shard_map/all_gather | solution.py:460
  896.3 17.8 all-reduce.24
  919.1 19.3 all-reduce.23
  949.2 37.3 %reduce-scatter.30.cloned.1.call-done = f32[256,2,512]{2,0,1:T(8,128)} async-done(((f32[1024,2,512]{2,0,1:T(8,128)}), f32[256,2,512]{2,0,1:T(8,128)}) %reduce-scatter.30.cloned.1.call-update) | async-done | bytes 1048592 | tf_op jit(solution)/shard_map/reduce_scatter | solution.py:73
  986.5 47.0 %reduce-scatter.38.cloned.1.call-done = f32[256,2,512]{2,0,1:T(8,128)} async-done(((f32[1024,2,512]{2,0,1:T(8,128)}), f32[256,2,512]{2,0,1:T(8,128)}) %reduce-scatter.38.cloned.1.call-update) | async-done | bytes 1048592 | tf_op jit(solution)/shard_map/reduce_scatter | solution.py:73
  1038.4 33.6 %all_gather.118 = bf16[512,512]{1,0:T(8,128)(2,1)} all-gather(bf16[64,512]{1,0:T(8,128)(2,1)} %param.29), channel_id=1, replica_groups=mesh['wide'=8,'narrow'=4] {'wide'}, dimensions={0}, use_global_device_ids=true | all-gather | bytes 589824 | tf_op jit(solution)/shard_map/all_gather | solution.py:463
  1072.0 33.6 %all_gather.119 = bf16[512,512]{0,1:T(8,128)(2,1)} all-gather(bf16[512,64]{0,1:T(8,128)(2,1)} %param.30), channel_id=1, replica_groups=mesh['wide'=8,'narrow'=4] {'wide'}, dimensions={1}, use_global_device_ids=true | all-gather | bytes 589824 | tf_op jit(solution)/shard_map/all_gather | solution.py:464
  1126.7 32.3 %reduce-scatter.32.cloned.1.call-done = f32[256,2,512]{2,0,1:T(8,128)} async-done(((f32[1024,2,512]{2,0,1:T(8,128)}), f32[256,2,512]{2,0,1:T(8,128)}) %reduce-scatter.32.cloned.1.call-update) | async-done | bytes 1048592 | tf_op jit(solution)/shard_map/reduce_scatter | solution.py:73
  1158.9 47.0 %reduce-scatter.40.cloned.1.call-done = f32[256,2,512]{2,0,1:T(8,128)} async-done(((f32[1024,2,512]{2,0,1:T(8,128)}), f32[256,2,512]{2,0,1:T(8,128)}) %reduce-scatter.40.cloned.1.call-update) | async-done | bytes 1048592 | tf_op jit(solution)/shard_map/reduce_scatter | solution.py:73
  1214.3 21.7 all-gather.34.cloned.1.call-done
  1270.9 36.3 %reduce-scatter.42.cloned.1.call-done = f32[256,2,512]{2,0,1:T(8,128)} async-done(((f32[1024,2,512]{2,0,1:T(8,128)}), f32[256,2,512]{2,0,1:T(8,128)}) %reduce-scatter.42.cloned.1.call-update) | async-done | bytes 1048592 | tf_op jit(solution)/shard_map/reduce_scatter | solution.py:81
  1307.2 47.0 %reduce-scatter.50.cloned.1.call-done = f32[256,2,512]{2,0,1:T(8,128)} async-done(((f32[1024,2,512]{2,0,1:T(8,128)}), f32[256,2,512]{2,0,1:T(8,128)}) %reduce-scatter.50.cloned.1.call-update) | async-done | bytes 1048592 | tf_op jit(solution)/shard_map/reduce_scatter | solution.py:81
  1387.9 20.3 all-gather.36.cloned.1.call-done
  1412.4 22.2 all-reduce.22
  1465.1 25.2 reduce-scatter.44.cloned.1.call-done
  1492.6 44.6 %reduce-scatter.52.cloned.1.call-done = f32[256,2,512]{2,0,1:T(8,128)} async-done(((f32[1024,2,512]{2,0,1:T(8,128)}), f32[256,2,512]{2,0,1:T(8,128)}) %reduce-scatter.52.cloned.1.call-update) | async-done | bytes 1048592 | tf_op jit(solution)/shard_map/reduce_scatter | solution.py:81
  1545.3 19.5 all-gather.38.cloned.1.call-done
  1837.7 42.7 %reduce-scatter.54.cloned.1.call-done = f32[256,2,512]{2,0,1:T(8,128)} async-done(((f32[1024,2,512]{2,0,1:T(8,128)}), f32[256,2,512]{2,0,1:T(8,128)}) %reduce-scatter.54.cloned.1.call-update) | async-done | bytes 1048592 | tf_op jit(solution)/shard_map/reduce_scatter | solution.py:81
  1967.3 37.6 %all-reduce.20 = f32[32,128]{1,0:T(8,128)S(1)} all-reduce(f32[32,128]{1,0:T(8,128)S(1)} %add.1374), channel_id=24, replica_groups=mesh['wide'=8,'narrow'=4] {'wide'}, use_global_device_ids=true, to_apply=%region_160.161.clone | all-reduce | flops 4096 | bytes 32768
  2068.0 23.4 reduce-scatter.56.cloned.1.call-done
  2097.9 41.2 %all-reduce.21 = (f32[5,512]{1,0:T(8,128)}, f32[9,512]{1,0:T(8,128)}, f32[5,512]{1,0:T(8,128)S(1)}, f32[2,2048]{1,0:T(2,128)S(1)}) all-reduce(f32[5,512]{1,0:T(8,128)S(1)} %add.1378, f32[9,512]{1,0:T(8,128)S(1)} %add.1379, f32[5,512]{1,0:T(8,128)S(1)} %maximum_add_fusion, ...), channel_id=1, replica_groups=mesh['wide'=8,'narrow'=4] {'wide','narrow'}, use_global_device_ids=true, to_apply=%region_174.175 | all-reduce | flops 13824 | bytes 110592 | tf_op jit(solution)/shard_map/psum | solution.py:642
  2140.3 19.4 reduce-scatter.72.cloned.1.call-done
  2159.6 67.1 %reduce-scatter.74.cloned.1.call-done = f32[512,64]{0,1:T(8,128)} async-done(((f32[512,512]{0,1:T(8,128)}), f32[512,64]{0,1:T(8,128)}) %reduce-scatter.74.cloned.1.call-update) | async-done | bytes 131088 | tf_op jit(solution)/shard_map/reduce_scatter | solution.py:659
  2226.8 64.8 %reduce-scatter.70.cloned.1.call-done = f32[128,64]{0,1:T(8,128)} async-done(((f32[128,512]{0,1:T(8,128)}), f32[128,64]{0,1:T(8,128)}) %reduce-scatter.70.cloned.1.call-update) | async-done | bytes 32784 | tf_op jit(solution)/shard_map/reduce_scatter | solution.py:657
  2291.5 64.9 %reduce-scatter.66.cloned.1.call-done = f32[128,64]{0,1:T(8,128)} async-done(((f32[128,512]{0,1:T(8,128)}), f32[128,64]{0,1:T(8,128)}) %reduce-scatter.66.cloned.1.call-update) | async-done | bytes 32784 | tf_op jit(solution)/shard_map/reduce_scatter | solution.py:654
  2356.4 65.0 %reduce-scatter.64.cloned.1.call-done = f32[64,128]{1,0:T(8,128)} async-done(((f32[512,128]{1,0:T(8,128)}), f32[64,128]{1,0:T(8,128)}) %reduce-scatter.64.cloned.1.call-update) | async-done | bytes 32784 | tf_op jit(solution)/shard_map/reduce_scatter | solution.py:653
  2421.5 66.8 %reduce-scatter.62.cloned.1.call-done = f32[64,3,128]{2,0,1:T(8,128)} async-done(((f32[512,3,128]{2,0,1:T(8,128)}), f32[64,3,128]{2,0,1:T(8,128)}) %reduce-scatter.62.cloned.1.call-update) | async-done | bytes 98320 | tf_op jit(solution)/shard_map/reduce_scatter | solution.py:652
  2488.3 67.2 %reduce-scatter.58.cloned.1.call-done = f32[64,512]{1,0:T(8,128)} async-done(((f32[512,512]{1,0:T(8,128)}), f32[64,512]{1,0:T(8,128)}) %reduce-scatter.58.cloned.1.call-update) | async-done | bytes 131088 | tf_op jit(solution)/shard_map/reduce_scatter | solution.py:650
  2555.5 67.2 %reduce-scatter.60.cloned.1.call-done = f32[512,64]{0,1:T(8,128)} async-done(((f32[512,512]{0,1:T(8,128)}), f32[512,64]{0,1:T(8,128)}) %reduce-scatter.60.cloned.1.call-update) | async-done | bytes 131088 | tf_op jit(solution)/shard_map/reduce_scatter | solution.py:651
  (1196 shorter events, 851.6 us)
Async XLA Ops:
  7.2 73.1 %all-gather.18.cloned.1.call-start = ((), (), s32[]{:S(2)}) async-start(), calls=%async_computation.25 | async-start | bytes 2621440 | tf_op jit(solution)/shard_map/all_gather | solution.py:69
  8.7 175.4 %copy-start.160 = (f32[1,512]{1,0:T(1,128)}, f32[1,512]{1,0:T(1,128)S(1)}, u32[]{:S(2)}) copy-start(f32[1,512]{1,0:T(1,128)S(1)} %get-tuple-element.323) | copy-start | bytes 6148
  12.3 169.4 %copy-start.26 = (bf16[1,256,2,512]{3,2,1,0:T(2,128)(2,1)}, bf16[1,256,2,512]{3,2,1,0:T(2,128)(2,1)S(1)}, u32[]{:S(2)}) copy-start(bf16[1,256,2,512]{3,2,1,0:T(2,128)(2,1)S(1)} %get-tuple-element.258) | copy-start | bytes 1572868
  12.3 169.3 %copy-start.28 = (bf16[1,256,2,512]{3,2,1,0:T(2,128)(2,1)}, bf16[1,256,2,512]{3,2,1,0:T(2,128)(2,1)S(1)}, u32[]{:S(2)}) copy-start(bf16[1,256,2,512]{3,2,1,0:T(2,128)(2,1)S(1)} %get-tuple-element.257) | copy-start | bytes 1572868
  14.6 74.1 %all-gather.26.cloned.1.call-start = ((), (), s32[]{:S(2)}) async-start(), calls=%async_computation.33 | async-start | bytes 2621440 | tf_op jit(solution)/shard_map/all_gather | solution.py:69
  15.3 119.3 %reduce-scatter.26.cloned.1.call-start = ((), (), s32[]{:S(2)}) async-start(), calls=%async_computation.26 | async-start | bytes 5242880 | tf_op jit(solution)/shard_map/reduce_scatter | solution.py:73
  88.7 92.9 %reduce-scatter.34.cloned.1.call-start = ((), (), s32[]{:S(2)}) async-start(), calls=%async_computation.34 | async-start | bytes 5242880 | tf_op jit(solution)/shard_map/reduce_scatter | solution.py:73
  97.0 256.3 %all-gather.20.cloned.1.call-start = ((), (), s32[]{:S(2)}) async-start(), calls=%async_computation.27 | async-start | bytes 2621440 | tf_op jit(solution)/shard_map/all_gather | solution.py:69
  185.9 171.8 %all-gather.28.cloned.1.call-start = ((), (), s32[]{:S(2)}) async-start(), calls=%async_computation.35 | async-start | bytes 2621440 | tf_op jit(solution)/shard_map/all_gather | solution.py:69
  186.5 551.3 %reduce-scatter.28.cloned.1.call-start = ((), (), s32[]{:S(2)}) async-start(), calls=%async_computation.28 | async-start | bytes 5242880 | tf_op jit(solution)/shard_map/reduce_scatter | solution.py:73
  256.2 99.7 %copy-start.9 = (bf16[2047,512]{0,1:T(8,128)(2,1)}, bf16[2047,512]{0,1:T(8,128)(2,1)S(1)}, u32[]{:S(2)}) copy-start(bf16[2047,512]{0,1:T(8,128)(2,1)S(1)} %convert_element_type.503) | copy-start | bytes 6288388
  452.5 91.0 %copy-start.153 = (f32[2,2,512]{2,1,0:T(2,128)}, f32[2,2,512]{2,1,0:T(2,128)S(1)}, u32[]{:S(2)}) copy-start(f32[2,2,512]{2,1,0:T(2,128)S(1)} %log_add_fusion.2) | copy-start | bytes 24580
  550.2 232.4 %reduce-scatter.36.cloned.1.call-start = ((), (), s32[]{:S(2)}) async-start(), calls=%async_computation.36 | async-start | bytes 5242880 | tf_op jit(solution)/shard_map/reduce_scatter | solution.py:73
  737.8 137.7 %all-gather.30.cloned.1.call-start = ((), (), s32[]{:S(2)}) async-start(), calls=%async_computation.37 | async-start | bytes 2621440 | tf_op jit(solution)/shard_map/all_gather | solution.py:69
  784.9 89.2 %copy-start.311 = (s32[2]{0:T(128)S(1)}, s32[2]{0:T(128)}, u32[]{:S(2)}) copy-start(s32[2]{0:T(128)} %copy-done.310) | copy-start | bytes 28
  787.0 92.5 %all-gather.22.cloned.1.call-start = ((), (), s32[]{:S(2)}) async-start(), calls=%async_computation.29 | async-start | bytes 2621440 | tf_op jit(solution)/shard_map/all_gather | solution.py:69
  787.6 199.0 %reduce-scatter.30.cloned.1.call-start = ((), (), s32[]{:S(2)}) async-start(), calls=%async_computation.30 | async-start | bytes 5242880 | tf_op jit(solution)/shard_map/reduce_scatter | solution.py:73
  945.5 88.0 %reduce-scatter.38.cloned.1.call-start = ((), (), s32[]{:S(2)}) async-start(), calls=%async_computation.38 | async-start | bytes 5242880 | tf_op jit(solution)/shard_map/reduce_scatter | solution.py:73
  949.1 156.5 %all-gather.24.cloned.1.call-start = ((), (), s32[]{:S(2)}) async-start(), calls=%async_computation.31 | async-start | bytes 2621440 | tf_op jit(solution)/shard_map/all_gather | solution.py:69
  1037.8 76.1 %all-gather.32.cloned.1.call-start = ((), (), s32[]{:S(2)}) async-start(), calls=%async_computation.39 | async-start | bytes 2621440 | tf_op jit(solution)/shard_map/all_gather | solution.py:69
  1038.4 120.6 %reduce-scatter.32.cloned.1.call-start = ((), (), s32[]{:S(2)}) async-start(), calls=%async_computation.32 | async-start | bytes 5242880 | tf_op jit(solution)/shard_map/reduce_scatter | solution.py:73
  1113.9 92.0 %reduce-scatter.40.cloned.1.call-start = ((), (), s32[]{:S(2)}) async-start(), calls=%async_computation.40 | async-start | bytes 5242880 | tf_op jit(solution)/shard_map/reduce_scatter | solution.py:73
  1122.2 113.8 %all-gather.34.cloned.1.call-start = ((), (), s32[]{:S(2)}) async-start(), calls=%async_computation.41 | async-start | bytes 2621440 | tf_op jit(solution)/shard_map/all_gather | solution.py:77
  1213.3 46.7 %all-gather.42.cloned.1.call-start = ((), (), s32[]{:S(2)}) async-start(), calls=%async_computation.49 | async-start | bytes 2621440 | tf_op jit(solution)/shard_map/all_gather | solution.py:77
  1213.9 93.3 %reduce-scatter.42.cloned.1.call-start = ((), (), s32[]{:S(2)}) async-start(), calls=%async_computation.42 | async-start | bytes 5242880 | tf_op jit(solution)/shard_map/reduce_scatter | solution.py:81
  1246.7 107.5 %reduce-scatter.50.cloned.1.call-start = ((), (), s32[]{:S(2)}) async-start(), calls=%async_computation.50 | async-start | bytes 5242880 | tf_op jit(solution)/shard_map/reduce_scatter | solution.py:81
  1270.8 113.2 %all-gather.44.cloned.1.call-start = ((), (), s32[]{:S(2)}) async-start(), calls=%async_computation.51 | async-start | bytes 2621440 | tf_op jit(solution)/shard_map/all_gather | solution.py:77
  1361.3 46.9 %all-gather.36.cloned.1.call-start = ((), (), s32[]{:S(2)}) async-start(), calls=%async_computation.43 | async-start | bytes 2621440 | tf_op jit(solution)/shard_map/all_gather | solution.py:77
  1367.8 122.5 %reduce-scatter.44.cloned.1.call-start = ((), (), s32[]{:S(2)}) async-start(), calls=%async_computation.44 | async-start | bytes 5242880 | tf_op jit(solution)/shard_map/reduce_scatter | solution.py:81
  1449.2 88.0 %reduce-scatter.52.cloned.1.call-start = ((), (), s32[]{:S(2)}) async-start(), calls=%async_computation.52 | async-start | bytes 5242880 | tf_op jit(solution)/shard_map/reduce_scatter | solution.py:81
  1465.0 99.8 %all-gather.38.cloned.1.call-start = ((), (), s32[]{:S(2)}) async-start(), calls=%async_computation.45 | async-start | bytes 2621440 | tf_op jit(solution)/shard_map/all_gather | solution.py:77
  1542.1 155.9 %all-gather.46.cloned.1.call-start = ((), (), s32[]{:S(2)}) async-start(), calls=%async_computation.53 | async-start | bytes 2621440 | tf_op jit(solution)/shard_map/all_gather | solution.py:77
  1545.3 290.5 %reduce-scatter.46.cloned.1.call-start = ((), (), s32[]{:S(2)}) async-start(), calls=%async_computation.46 | async-start | bytes 5242880 | tf_op jit(solution)/shard_map/reduce_scatter | solution.py:81
  1595.5 97.7 %copy-start.141 = (bf16[1024,2,1,128]{3,0,2,1:T(8,128)(2,1)}, bf16[1024,2,1,128]{3,0,2,1:T(8,128)(2,1)S(1)}, u32[]{:S(2)}) copy-start(bf16[1024,2,1,128]{3,0,2,1:T(8,128)(2,1)S(1)} %copy.202) | copy-start | bytes 1572868
  1697.9 182.6 %reduce-scatter.54.cloned.1.call-start = ((), (), s32[]{:S(2)}) async-start(), calls=%async_computation.54 | async-start | bytes 5242880 | tf_op jit(solution)/shard_map/reduce_scatter | solution.py:81
  1835.8 71.8 %all-gather.40.cloned.1.call-start = ((), (), s32[]{:S(2)}) async-start(), calls=%async_computation.47 | async-start | bytes 2621440 | tf_op jit(solution)/shard_map/all_gather | solution.py:77
  1884.9 47.3 %all-gather.48.cloned.1.call-start = ((), (), s32[]{:S(2)}) async-start(), calls=%async_computation.55 | async-start | bytes 2621440 | tf_op jit(solution)/shard_map/all_gather | solution.py:77
  1888.5 161.6 %reduce-scatter.68.cloned.1.call-start = ((), (), s32[]{:S(2)}) async-start(), calls=%async_computation.62 | async-start | bytes 589824 | tf_op jit(solution)/shard_map/reduce_scatter | solution.py:655
  1892.7 173.3 %reduce-scatter.48.cloned.1.call-start = ((), (), s32[]{:S(2)}) async-start(), calls=%async_computation.48 | async-start | bytes 5242880 | tf_op jit(solution)/shard_map/reduce_scatter | solution.py:81
  1916.6 174.8 %reduce-scatter.56.cloned.1.call-start = ((), (), s32[]{:S(2)}) async-start(), calls=%async_computation.56 | async-start | bytes 5242880 | tf_op jit(solution)/shard_map/reduce_scatter | solution.py:81
  1941.3 218.3 %reduce-scatter.72.cloned.1.call-start = ((), (), s32[]{:S(2)}) async-start(), calls=%async_computation.64 | async-start | bytes 1179648 | tf_op jit(solution)/shard_map/reduce_scatter | solution.py:658
  1947.4 279.3 %reduce-scatter.74.cloned.1.call-start = ((), (), s32[]{:S(2)}) async-start(), calls=%async_computation.65 | async-start | bytes 1179648 | tf_op jit(solution)/shard_map/reduce_scatter | solution.py:659
  1956.4 335.1 %reduce-scatter.70.cloned.1.call-start = ((), (), s32[]{:S(2)}) async-start(), calls=%async_computation.63 | async-start | bytes 294912 | tf_op jit(solution)/shard_map/reduce_scatter | solution.py:657
  2011.7 344.7 %reduce-scatter.66.cloned.1.call-start = ((), (), s32[]{:S(2)}) async-start(), calls=%async_computation.61 | async-start | bytes 294912 | tf_op jit(solution)/shard_map/reduce_scatter | solution.py:654
  2036.1 385.4 %reduce-scatter.64.cloned.1.call-start = ((), (), s32[]{:S(2)}) async-start(), calls=%async_computation.60 | async-start | bytes 294912 | tf_op jit(solution)/shard_map/reduce_scatter | solution.py:653
  2042.7 445.6 %reduce-scatter.62.cloned.1.call-start = ((), (), s32[]{:S(2)}) async-start(), calls=%async_computation.59 | async-start | bytes 884736 | tf_op jit(solution)/shard_map/reduce_scatter | solution.py:652
  2048.6 507.0 %reduce-scatter.58.cloned.1.call-start = ((), (), s32[]{:S(2)}) async-start(), calls=%async_computation.57 | async-start | bytes 1179648 | tf_op jit(solution)/shard_map/reduce_scatter | solution.py:650
  2058.3 564.4 %reduce-scatter.60.cloned.1.call-start = ((), (), s32[]{:S(2)}) async-start(), calls=%async_computation.58 | async-start | bytes 1179648 | tf_op jit(solution)/shard_map/reduce_scatter | solution.py:651
  (381 other events, 3533.7 us)
Sparse Core Ops, SparseCore 0:
  14.7 25.2 all-gather.17
  42.2 22.5 all-gather.25
  88.8 45.7 reduce-scatter.25
  137.0 44.5 reduce-scatter.33
  186.0 22.6 all-gather.19
  210.2 22.5 all-gather.27
  550.3 44.6 reduce-scatter.27
  737.9 44.6 reduce-scatter.35
  787.1 22.5 all-gather.29
  811.7 22.5 all-gather.21
  945.6 40.8 reduce-scatter.29
  988.9 44.5 reduce-scatter.37
  1037.9 22.5 all-gather.23
  1061.9 22.5 all-gather.31
  1114.0 44.8 reduce-scatter.31
  1161.3 44.5 reduce-scatter.39
  1213.4 22.5 all-gather.33
  1237.4 22.5 all-gather.41
  1262.6 44.5 reduce-scatter.41
  1309.6 44.5 reduce-scatter.49
  1361.5 22.5 all-gather.43
  1385.6 22.5 all-gather.35
  1449.4 40.8 reduce-scatter.43
  1492.7 44.5 reduce-scatter.51
  1542.2 22.5 all-gather.37
  1566.2 22.5 all-gather.45
  1698.0 44.7 reduce-scatter.45
  1835.9 44.5 reduce-scatter.53
  1885.0 22.5 all-gather.39
  1909.6 22.5 all-gather.47
  1935.5 62.6 reduce-scatter.67
  2000.8 43.5 reduce-scatter.47
  2046.7 44.5 reduce-scatter.55
  2095.3 64.2 reduce-scatter.71
  2163.6 63.1 reduce-scatter.73
  2230.5 60.9 reduce-scatter.69
  2295.3 61.1 reduce-scatter.65
  2360.3 61.1 reduce-scatter.63
  2425.2 63.0 reduce-scatter.61
  2492.3 63.2 reduce-scatter.57
  2559.5 63.1 reduce-scatter.59
where the time goes:
time: 2640 us; the launch traced here: 2630 us
  waiting for transfers between devices  1120 us (42%)
  local copies, waits for them, and re-layouts  530 us (20%)
  blocking collectives  448 us (17%)
  matrix products  298 us (11%)
  other arithmetic  210 us (8%)
    reduce_scatter x8, waiting for transfers between devices, fold_rows(): lax.psum_scatter(partial_sums, 'narrow', scatter_dimension=0, tiled=True)  293 us
    reduce_scatter x8, waiting for transfers between devices, fold_grads(): lax.psum_scatter(partial_sums, 'narrow', scatter_dimension=0, tiled=True)  219 us
    all_gather x8, waiting for transfers between devices, spread_grads(): return lax.all_gather(values_in, 'narrow', axis=0, tiled=True)  121 us
    reshape x4, local copies, waits for them, and re-layouts, shift_rows(): flattened.reshape(block_rows, block_rows + key_count - 1)[:, :key_count]  104 us
    reshape x4, local copies, waits for them, and re-layouts, shift_rows(): flattened = padded.reshape(-1)  87.4 us
    reduce_scatter x1, waiting for transfers between devices, shards(): lax.psum_scatter(ffn_parts[0], 'wide', scatter_dimension=0, tiled=True)  67.2 us
    reduce_scatter x1, waiting for transfers between devices, shards(): lax.psum_scatter(ffn_parts[1], 'wide', scatter_dimension=1, tiled=True)  67.2 us
    reduce_scatter x1, waiting for transfers between devices, shards(): lax.psum_scatter(ffn_parts[3], 'wide', scatter_dimension=1, tiled=True)  67.1 us
  transfers between devices with their start and end apart: 41, of which 28 were waited for; matrix products, arithmetic and copies ran while one was open for 28% of the time, Pallas kernels for 0%

commit v1 on v0

v1 whole, which is shorter than its diff:
```python
from functools import partial
import math

import jax
import jax.numpy as jnp
import numpy as np
from jax import lax
from jax.experimental import pallas as pl
from jax.experimental.pallas import tpu as pltpu
from jax.sharding import PartitionSpec as P

HEAD_DIM = 64
EPSILON = 1e-05
MASKED = -1e30
LANES = 128
ROWS = 256
CONV_ROWS = 128
SMALL_ROWS = 15
BF = jnp.bfloat16
F32 = jnp.float32
NN = (((1,), (0,)), ((), ()))
NT = (((1,), (1,)), ((), ()))


def dot(left, right, dims=NN):
    return lax.dot_general(left, right, dims, preferred_element_type=F32)


def sigmoid(values):
    return 0.5 * jnp.tanh(0.5 * values) + 0.5


def normal_rows(values):
    center = values - jnp.mean(values, axis=-1, keepdims=True)
    inverse = lax.rsqrt(jnp.mean(center * center, axis=-1, keepdims=True) + EPSILON)
    return center * inverse, inverse


def normal_rows_back(upstream, normal, inverse, gain):
    scaled = upstream * gain
    plain = jnp.mean(scaled, axis=-1, keepdims=True)
    cross = jnp.mean(scaled * normal, axis=-1, keepdims=True)
    return inverse * (scaled - plain - normal * cross)


def column_sum(values):
    return jnp.sum(values, axis=0, keepdims=True)


def chunk(index, rows=ROWS):
    return pl.ds(pl.multiple_of(index * rows, rows), rows)


def first_step(axis_step):
    return pl.when(axis_step == 0)


def full(shape):
    return pl.BlockSpec(shape, lambda *_: (0,) * len(shape), pipeline_mode=pl.Buffered(1))


def params(**more):
    return pltpu.CompilerParams(vmem_limit_bytes=62 * 1024 * 1024, **more)


def ffn_forward_kernel(x_ref, gain_ref, bias_ref, w_ref, hidden_ref, out_ref, a_ref, h_ref):
    step = pl.program_id(0)
    count = x_ref.shape[0] // ROWS
    width = a_ref.shape[1]

    @pl.when(step == 0)
    def _():
        @pl.loop(0, count)
        def _(i):
            rows = chunk(i)
            normal, _ = normal_rows(x_ref[rows, :].astype(F32))
            h_ref[rows, :] = (normal * gain_ref[0:1, :] + bias_ref[0:1, :]).astype(BF)
            out_ref[rows, :] = jnp.zeros((ROWS, out_ref.shape[1]), F32)

    @pl.loop(0, count)
    def _(i):
        rows = chunk(i)
        pre = dot(h_ref[rows, :], w_ref[:, :width]) + hidden_ref[0:1, :]
        a_ref[rows, :] = pre.astype(BF)
        act = (pre * sigmoid(pre)).astype(BF)
        out_ref[rows, :] += dot(act, w_ref[:, width:], NT)

    @pl.when(step == pl.num_programs(0) - 1)
    def _():
        @pl.loop(0, count)
        def _(i):
            rows = chunk(i)
            out_ref[rows, :] = x_ref[rows, :].astype(F32) + 0.5 * (
                out_ref[rows, :] + bias_ref[5:6, :]
            )


def ffn_forward(x, gains, biases, weights, hidden):
    length, features = x.shape
    blocks = weights.shape[0] // features
    width = hidden.shape[1] // blocks
    return pl.pallas_call(
        ffn_forward_kernel,
        name="ffn_forward",
        grid=(blocks,),
        in_specs=[
            full(x.shape),
            full(gains.shape),
            full(biases.shape),
            pl.BlockSpec((features, 2 * width), lambda n: (n, 0)),
            pl.BlockSpec((2, width), lambda n: (0, n)),
        ],
        out_specs=[
            full((length, features)),
            pl.BlockSpec((length, width), lambda n: (0, n)),
        ],
        out_shape=[
            jax.ShapeDtypeStruct((length, features), F32),
            jax.ShapeDtypeStruct((length, blocks * width), BF),
        ],
        scratch_shapes=[pltpu.VMEM((length, features), BF)],
        compiler_params=params(),
    )(x, gains, biases, weights, hidden)


def ffn_backward_kernel(
    up_ref, x_ref, gain_ref, bias_ref, w_ref, a_ref,
    out_ref, grad_ref, hidden_grad_ref, vec_ref,
    ht_ref, df_ref, dft_ref, s_ref, da_ref,
):
    step = pl.program_id(0)
    length, features = x_ref.shape
    count = length // ROWS
    width = a_ref.shape[1]

    @pl.when(step == 0)
    def _():
        vec_ref[...] = jnp.zeros(vec_ref.shape, F32)

        @pl.loop(0, count)
        def _(i):
            rows = chunk(i)
            normal, _ = normal_rows(x_ref[rows, :].astype(F32))
            hidden = normal * gain_ref[0:1, :] + bias_ref[0:1, :]
            ht_ref[:, rows] = hidden.T.astype(BF)
            half = 0.5 * up_ref[rows, :]
            df_ref[rows, :] = half.astype(BF)
            dft_ref[:, rows] = half.T.astype(BF)
            vec_ref[2:3, :] += column_sum(half)
            out_ref[rows, :] = jnp.zeros((ROWS, features), F32)

    hidden_grad_ref[...] = jnp.zeros(hidden_grad_ref.shape, F32)

    @pl.loop(0, count)
    def _(i):
        rows = chunk(i)
        pre = a_ref[rows, :].astype(F32)
        sigma = sigmoid(pre)
        s_ref[rows, :] = (pre * sigma).astype(BF)
        grad_act = dot(df_ref[rows, :], w_ref[:, width:])
        grad_pre = (grad_act * (sigma * (1.0 + pre * (1.0 - sigma)))).astype(BF)
        da_ref[rows, :] = grad_pre
        hidden_grad_ref[...] += column_sum(grad_pre.astype(F32))
        out_ref[rows, :] += dot(grad_pre, w_ref[:, :width], NT)

    @pl.loop(0, features // LANES)
    def _(i):
        rows = chunk(i, LANES)
        grad_ref[rows, :width] = dot(ht_ref[rows, :], da_ref[...]).astype(BF)
        grad_ref[rows, width:] = dot(dft_ref[rows, :], s_ref[...]).astype(BF)

    @pl.when(step == pl.num_programs(0) - 1)
    def _():
        @pl.loop(0, count)
        def _(i):
            rows = chunk(i)
            grad_normed = out_ref[rows, :]
            normal, inverse = normal_rows(x_ref[rows, :].astype(F32))
            vec_ref[0:1, :] += column_sum(grad_normed * normal)
            vec_ref[1:2, :] += column_sum(grad_normed)
            out_ref[rows, :] = up_ref[rows, :] + normal_rows_back(
                grad_normed, normal, inverse, gain_ref[0:1, :]
            )


def ffn_backward(upstream, x, gains, biases, weights, a_saved, grads):
    length, features = x.shape
    blocks = weights.shape[0] // features
    width = a_saved.shape[1] // blocks

    def kernel(up, xr, g, b, w, a, grads_in, *rest):
        ffn_backward_kernel(up, xr, g, b, w, a, *rest)

    return pl.pallas_call(
        kernel,
        name="ffn_backward",
        grid=(blocks,),
        in_specs=[
            full(upstream.shape),
            full(x.shape),
            full(gains.shape),
            full(biases.shape),
            pl.BlockSpec((features, 2 * width), lambda n: (n, 0)),
            pl.BlockSpec((length, width), lambda n: (0, n)),
            pl.BlockSpec(memory_space=pl.ANY),
        ],
        out_specs=[
            full((length, features)),
            pl.BlockSpec((features, 2 * width), lambda n: (n, 0)),
            pl.BlockSpec((1, width), lambda n: (0, n)),
            full((8, features)),
        ],
        out_shape=[
            jax.ShapeDtypeStruct((length, features), F32),
            jax.ShapeDtypeStruct(grads.shape, BF),
            jax.ShapeDtypeStruct((1, blocks * width), F32),
            jax.ShapeDtypeStruct((8, features), F32),
        ],
        scratch_shapes=[
            pltpu.VMEM((features, length), BF),
            pltpu.VMEM((length, features), BF),
            pltpu.VMEM((features, length), BF),
            pltpu.VMEM((length, width), BF),
            pltpu.VMEM((length, width), BF),
        ],
        input_output_aliases={6: 1},
        compiler_params=params(),
    )(upstream, x, gains, biases, weights, a_saved, grads)


def attention_forward_kernel(
    x_ref, gain_ref, bias_ref, w_ref, unit_ref, table_ref, masked_ref,
    out_ref, h_ref, qc_ref, qp_ref, k_ref, v_ref, pos_ref, ctx_ref, p_ref,
):
    step = pl.program_id(0)
    length, features = x_ref.shape
    count = length // ROWS
    window = length + ROWS
    scale = 1.0 / math.sqrt(HEAD_DIM)

    @pl.when(step == 0)
    def _():
        @pl.loop(0, count)
        def _(i):
            rows = chunk(i)
            values = x_ref[rows, :]
            normal, _ = normal_rows(values)
            h_ref[rows, :] = (normal * gain_ref[1:2, :] + bias_ref[1:2, :]).astype(BF)
            out_ref[rows, :] = values + bias_ref[6:7, :]

    @pl.loop(0, count)
    def _(i):
        rows = chunk(i)
        project = dot(h_ref[rows, :], w_ref[:, : 3 * LANES])
        query = project[:, :LANES]
        qc_ref[rows, :] = ((query + unit_ref[1:2, :]).astype(BF) * scale).astype(BF)
        qp_ref[rows, :] = ((query + unit_ref[2:3, :]).astype(BF) * scale).astype(BF)
        k_ref[rows, :] = project[:, LANES : 2 * LANES].astype(BF)
        v_ref[rows, :] = (project[:, 2 * LANES :] + unit_ref[0:1, :]).astype(BF)

    @pl.loop(0, 2 * count)
    def _(i):
        rows = chunk(i)
        pos_ref[rows, :] = dot(table_ref[rows, :], w_ref[:, 3 * LANES : 4 * LANES]).astype(BF)

    lane = lax.broadcasted_iota(jnp.int32, (ROWS, LANES), 1) < HEAD_DIM

    @pl.loop(0, count)
    def _(i):
        rows = chunk(i)
        begin = pl.multiple_of((length - ROWS) - i * ROWS, ROWS)
        positions = pos_ref[pl.ds(begin, window), :]
        results = []
        for head in range(2):
            own = lane if head == 0 else jnp.logical_not(lane)
            rows_c = jnp.where(own, qc_ref[rows, :], jnp.zeros((), BF))
            rows_p = jnp.where(own, qp_ref[rows, :], jnp.zeros((), BF))
            raw = dot(rows_p, positions, NT)
            shifted = pltpu.roll(raw, length + 1, 1, stride=1, stride_axis=0)[:, :length]
            scores = dot(rows_c, k_ref[...], NT) + shifted + masked_ref[...]
            top = jnp.max(scores, axis=1, keepdims=True)
            powers = jnp.exp(scores - top)
            inverse = 1.0 / jnp.sum(powers, axis=1, keepdims=True)
            probs = (powers * inverse).astype(BF)
            p_ref[head, rows, :] = probs
            results.append(dot(probs, v_ref[...]))
        context = jnp.where(lane, results[0], results[1])
        ctx_ref[rows, :] = context
        out_ref[rows, :] += dot(context.astype(BF), w_ref[:, 4 * LANES :], NT)


def attention_forward(x, gains, biases, weights, units, table, masked):
    length, features = x.shape
    blocks = weights.shape[0] // features
    column = pl.BlockSpec((length, LANES), lambda n: (0, n))
    low = jax.ShapeDtypeStruct((length, features), BF)
    return pl.pallas_call(
        attention_forward_kernel,
        name="attention_forward",
        grid=(blocks,),
        in_specs=[
            full(x.shape),
            full(gains.shape),
            full(biases.shape),
            pl.BlockSpec((features, 5 * LANES), lambda n: (n, 4)),
            pl.BlockSpec((5, LANES), lambda n: (0, n)),
            full(table.shape),
            full(masked.shape),
        ],
        out_specs=[
            full((length, features)),
            full((length, features)),
            column,
            column,
            column,
            column,
            pl.BlockSpec((2 * length, LANES), lambda n: (0, n)),
            column,
            pl.BlockSpec((2, length, length), lambda n: (n, 0, 0)),
        ],
        out_shape=[
            jax.ShapeDtypeStruct((length, features), F32),
            low,
            low,
            low,
            low,
            low,
            jax.ShapeDtypeStruct((2 * length, features), BF),
            jax.ShapeDtypeStruct((length, features), F32),
            jax.ShapeDtypeStruct((2 * blocks, length, length), BF),
        ],
        compiler_params=params(),
    )(x, gains, biases, weights, units, table, masked)


def attention_backward_kernel(
    up_ref, x_ref, h_ref, gain_ref, w_ref, qc_ref, qp_ref, k_ref, v_ref, pos_ref, ctx_ref, p_ref,
    table_ref,
    out_ref, grad_ref, unit_ref, vec_ref,
    do_ref, dot_ref, ht_ref, dqkv_ref, dvt_ref, dkt_ref, dpt_ref,
):
    step = pl.program_id(0)
    length, features = x_ref.shape
    count = length // ROWS
    window = length + ROWS
    scale = 1.0 / math.sqrt(HEAD_DIM)

    @pl.when(step == 0)
    def _():
        vec_ref[...] = jnp.zeros(vec_ref.shape, F32)

        @pl.loop(0, count)
        def _(i):
            rows = chunk(i)
            upstream = up_ref[rows, :]
            do_ref[rows, :] = upstream.astype(BF)
            dot_ref[:, rows] = upstream.T.astype(BF)
            ht_ref[:, rows] = h_ref[rows, :].astype(F32).T.astype(BF)
            out_ref[rows, :] = jnp.zeros((ROWS, features), F32)

    dvt_ref[...] = jnp.zeros(dvt_ref.shape, F32)
    dkt_ref[...] = jnp.zeros(dkt_ref.shape, F32)
    dpt_ref[...] = jnp.zeros(dpt_ref.shape, F32)
    unit_ref[...] = jnp.zeros(unit_ref.shape, F32)

    lane = lax.broadcasted_iota(jnp.int32, (ROWS, LANES), 1) < HEAD_DIM
    mirror = (
        lax.broadcasted_iota(jnp.int32, (ROWS, ROWS), 0)
        + lax.broadcasted_iota(jnp.int32, (ROWS, ROWS), 1)
        == ROWS - 1
    ).astype(BF)
    blank = jnp.zeros((ROWS, ROWS), BF)

    @pl.loop(0, count)
    def _(i):
        rows = chunk(i)
        begin = pl.multiple_of((length - ROWS) - i * ROWS, ROWS)
        span = pl.ds(begin, window)
        positions = pos_ref[span, :]
        grad_f32 = dot(do_ref[rows, :], w_ref[:, 4 * LANES :])
        grad_ctx = grad_f32.astype(BF)
        wide_ctx = grad_ctx.astype(F32)
        weighted = wide_ctx * ctx_ref[rows, :]
        grad_ctx_t = wide_ctx.T.astype(BF)
        qc_t = qc_ref[rows, :].astype(F32).T.astype(BF)
        qp_t = dot(qp_ref[rows, :].astype(F32).T.astype(BF), mirror).astype(BF)
        from_keys = []
        from_pos = []
        for head in range(2):
            own = lane if head == 0 else jnp.logical_not(lane)
            part = slice(head * HEAD_DIM, (head + 1) * HEAD_DIM)
            center = jnp.sum(jnp.where(own, weighted, 0.0), axis=1, keepdims=True)
            grad_probs = dot(jnp.where(own, grad_ctx, jnp.zeros((), BF)), v_ref[...], NT)
            probs = p_ref[head, rows, :]
            grad_scores = (probs.astype(F32) * (grad_probs - center)).astype(BF)
            dvt_ref[part, :] += dot(grad_ctx_t[part, :], probs)
            dkt_ref[part, :] += dot(qc_t[part, :], grad_scores)
            from_keys.append(dot(grad_scores, k_ref[...]))
            flipped = dot(mirror, grad_scores).astype(BF)
            spread = pltpu.roll(
                jnp.concatenate([flipped, blank], axis=1), 0, 1, stride=1, stride_axis=0
            )
            dpt_ref[part, span] += dot(qp_t[part, :], spread)
            from_pos.append(dot(spread, positions))
        grad_c = jnp.where(lane, from_keys[0], from_keys[1]) * scale
        turned = (jnp.where(lane, from_pos[0], from_pos[1]) * scale).astype(BF)
        grad_p = dot(mirror, turned)
        dqkv_ref[rows, :LANES] = (grad_c + grad_p).astype(BF)
        unit_ref[1:2, :] += column_sum(grad_c)
        unit_ref[2:3, :] += column_sum(grad_p)

    @pl.loop(0, count)
    def _(i):
        rows = chunk(i)
        dqkv_ref[rows, LANES : 2 * LANES] = dkt_ref[:, rows].T.astype(BF)
        grad_value = dvt_ref[:, rows].T.astype(BF)
        dqkv_ref[rows, 2 * LANES :] = grad_value
        unit_ref[0:1, :] += column_sum(grad_value.astype(F32))
        out_ref[rows, :] += dot(dqkv_ref[rows, :], w_ref[:, : 3 * LANES], NT)

    @pl.loop(0, features // LANES)
    def _(i):
        rows = chunk(i, LANES)
        grad_ref[rows, : 3 * LANES] = dot(ht_ref[rows, :], dqkv_ref[...]).astype(BF)
        grad_ref[rows, 4 * LANES :] = dot(dot_ref[rows, :], ctx_ref[...].astype(BF)).astype(BF)

    grad_pos = dot(dpt_ref[...].astype(BF), table_ref[...])
    grad_ref[:, 3 * LANES : 4 * LANES] = grad_pos.T.astype(BF)

    @pl.when(step == pl.num_programs(0) - 1)
    def _():
        @pl.loop(0, count)
        def _(i):
            rows = chunk(i)
            grad_normed = out_ref[rows, :]
            normal, inverse = normal_rows(x_ref[rows, :])
            vec_ref[0:1, :] += column_sum(grad_normed * normal)
            vec_ref[1:2, :] += column_sum(grad_normed)
            out_ref[rows, :] = up_ref[rows, :] + normal_rows_back(
                grad_normed, normal, inverse, gain_ref[1:2, :]
            )


def attention_backward(upstream, x, saved, gains, weights, table, grads):
    normed, qc, qp, keys, values, pos, context, probs = saved
    length, features = x.shape
    blocks = weights.shape[0] // features
    column = pl.BlockSpec((length, LANES), lambda n: (0, n))

    def kernel(*refs):
        attention_backward_kernel(*refs[:13], *refs[14:])

    return pl.pallas_call(
        kernel,
        name="attention_backward",
        grid=(blocks,),
        in_specs=[
            full(upstream.shape),
            full(x.shape),
            full(normed.shape),
            full(gains.shape),
            pl.BlockSpec((features, 5 * LANES), lambda n: (n, 4)),
            column,
            column,
            column,
            column,
            pl.BlockSpec((2 * length, LANES), lambda n: (0, n)),
            column,
            pl.BlockSpec((2, length, length), lambda n: (n, 0, 0)),
            full(table.shape),
            pl.BlockSpec(memory_space=pl.ANY),
        ],
        out_specs=[
            full((length, features)),
            pl.BlockSpec((features, 5 * LANES), lambda n: (n, 4)),
            pl.BlockSpec((8, LANES), lambda n: (0, n)),
            full((8, features)),
        ],
        out_shape=[
            jax.ShapeDtypeStruct((length, features), F32),
            jax.ShapeDtypeStruct(grads.shape, BF),
            jax.ShapeDtypeStruct((8, features), F32),
            jax.ShapeDtypeStruct((8, features), F32),
        ],
        scratch_shapes=[
            pltpu.VMEM((length, features), BF),
            pltpu.VMEM((features, length), BF),
            pltpu.VMEM((features, length), BF),
            pltpu.VMEM((length, 3 * LANES), BF),
            pltpu.VMEM((LANES, length), F32),
            pltpu.VMEM((LANES, length), F32),
            pltpu.VMEM((LANES, 2 * length), F32),
        ],
        input_output_aliases={13: 1},
        compiler_params=params(),
    )(upstream, x, normed, gains, weights, qc, qp, keys, values, pos, context, probs, table, grads)


def tap_selector(tap_count, features, wide_count, transposed):
    shape = (features, tap_count) if transposed else (tap_count, features)
    row = lax.broadcasted_iota(jnp.int32, shape, 0 if transposed else 1)
    tap = lax.broadcasted_iota(jnp.int32, shape, 1 if transposed else 0)
    per = tap_count // wide_count
    place = tap // per * (features // wide_count) + lax.rem(tap, per)
    return (row == place).astype(BF)


def valid_rows(begin, rows, length_here):
    index = lax.broadcasted_iota(jnp.int32, (rows, 1), 0) + begin
    return (index < length_here).astype(F32)


def conv_forward_kernel(
    taps, wide_count, len_ref, x_ref, gain_ref, bias_ref, w_ref, unit_ref,
    h_ref, z_ref, mixed_ref, stat_ref,
    pad_ref, tap_ref,
):
    step = pl.program_id(0)
    length, features = x_ref.shape
    count = length // ROWS
    half = taps // 2
    valid = len_ref[0]

    @pl.when(step == 0)
    def _():
        @pl.loop(0, count)
        def _(i):
            rows = chunk(i)
            normal, _ = normal_rows(x_ref[rows, :])
            h_ref[rows, :] = (normal * gain_ref[2:3, :] + bias_ref[2:3, :]).astype(BF)
        pad_ref[:half, :] = jnp.zeros((half, LANES), F32)
        pad_ref[half + length :, :] = jnp.zeros((half, LANES), F32)

    tap_ref[...] = dot(tap_selector(taps, features, wide_count, False), w_ref[:, 3 * LANES :])

    @pl.loop(0, count)
    def _(i):
        rows = chunk(i)
        z = dot(h_ref[rows, :], w_ref[:, : 2 * LANES])
        value = z[:, :LANES] + unit_ref[3:4, :]
        gate = z[:, LANES:] + unit_ref[4:5, :]
        z_ref[rows, :LANES] = value.astype(BF)
        z_ref[rows, LANES:] = gate.astype(BF)
        glu = value * sigmoid(gate) * valid_rows(i * ROWS, ROWS, valid)
        pad_ref[pl.ds(pl.multiple_of(i * ROWS + half, 8), ROWS), :] = glu

    stat_ref[...] = jnp.zeros(stat_ref.shape, F32)

    @pl.loop(0, length // CONV_ROWS)
    def _(i):
        rows = chunk(i, CONV_ROWS)
        area = pad_ref[pl.ds(pl.multiple_of(i * CONV_ROWS, CONV_ROWS), CONV_ROWS + taps), :]
        total = jnp.zeros((CONV_ROWS, LANES), F32)
        for shift in range(8):
            moved = area[shift : shift + CONV_ROWS + taps - 8, :]
            for group in range(taps // 8):
                tap = 8 * group + shift - 1
                if tap >= 0:
                    total += tap_ref[tap : tap + 1, :] * moved[8 * group : 8 * group + CONV_ROWS, :]
        total += tap_ref[taps - 1 : taps, :] * area[taps : taps + CONV_ROWS, :]
        mixed_ref[rows, :] = total
        mask = valid_rows(i * CONV_ROWS, CONV_ROWS, valid)
        stat_ref[0:1, :] += column_sum(total * mask)

    mean = stat_ref[0:1, :] / valid.astype(F32)
    stat_ref[0:1, :] = mean

    @pl.loop(0, count)
    def _(i):
        rows = chunk(i)
        center = mixed_ref[rows, :] - mean
        stat_ref[1:2, :] += column_sum(center * center * valid_rows(i * ROWS, ROWS, valid))


def conv_forward(taps, wide_count, valid, x, gains, biases, weights, units):
    length, features = x.shape
    blocks = weights.shape[0] // features
    return pl.pallas_call(
        partial(conv_forward_kernel, taps, wide_count),
        name="conv_forward",
        grid=(blocks,),
        in_specs=[
            pl.BlockSpec(memory_space=pltpu.SMEM),
            full(x.shape),
            full(gains.shape),
            full(biases.shape),
            pl.BlockSpec((features, 4 * LANES), lambda n: (n, 4)),
            pl.BlockSpec((5, LANES), lambda n: (0, n)),
        ],
        out_specs=[
            full((length, features)),
            pl.BlockSpec((length, 2 * LANES), lambda n: (0, n)),
            pl.BlockSpec((length, LANES), lambda n: (0, n)),
            pl.BlockSpec((8, LANES), lambda n: (0, n)),
        ],
        out_shape=[
            jax.ShapeDtypeStruct((length, features), BF),
            jax.ShapeDtypeStruct((length, 2 * features), BF),
            jax.ShapeDtypeStruct((length, features), F32),
            jax.ShapeDtypeStruct((8, features), F32),
        ],
        scratch_shapes=[
            pltpu.VMEM((length + taps, LANES), F32),
            pltpu.VMEM((taps, LANES), F32),
        ],
        compiler_params=params(),
    )(valid, x, gains, biases, weights, units)


def conv_backward_kernel(
    taps, wide_count,
    len_ref, up_ref, x_ref, h_ref, gain_ref, w_ref, z_ref, mixed_ref, dbn_ref, stat_ref, affine_ref,
    out_grad_ref,
    out_ref, grad_ref, unit_ref, vec_ref,
    glu_ref, dmix_ref, tap_ref, dz_ref, ht_ref, acc_ref,
):
    step = pl.program_id(0)
    length, features = x_ref.shape
    count = length // ROWS
    half = taps // 2
    valid = len_ref[0]

    @pl.when(step == 0)
    def _():
        vec_ref[...] = jnp.zeros(vec_ref.shape, F32)

        @pl.loop(0, count)
        def _(i):
            rows = chunk(i)
            ht_ref[:, rows] = h_ref[rows, :].astype(F32).T.astype(BF)
            out_ref[rows, :] = jnp.zeros((ROWS, features), F32)
        blank = jnp.zeros((half, LANES), F32)
        glu_ref[:half, :] = blank
        glu_ref[half + length :, :] = blank
        dmix_ref[:half, :] = blank
        dmix_ref[half + length :, :] = blank

    tap_ref[...] = dot(tap_selector(taps, features, wide_count, False), w_ref[:, 3 * LANES :])

    mean = stat_ref[0:1, :]
    inverse = stat_ref[1:2, :]
    plain = stat_ref[2:3, :]
    cross = stat_ref[3:4, :]
    factor = inverse * affine_ref[0:1, :]

    @pl.loop(0, count)
    def _(i):
        rows = chunk(i)
        mask = valid_rows(i * ROWS, ROWS, valid)
        normal = (mixed_ref[rows, :] - mean) * inverse
        place = pl.ds(pl.multiple_of(i * ROWS + half, 8), ROWS)
        dmix_ref[place, :] = factor * (dbn_ref[rows, :] - mask * (plain + normal * cross))
        value = z_ref[rows, :LANES].astype(F32)
        gate = z_ref[rows, LANES:].astype(F32)
        glu_ref[place, :] = value * sigmoid(gate) * mask

    acc_ref[...] = jnp.zeros(acc_ref.shape, F32)
    unit_ref[...] = jnp.zeros(unit_ref.shape, F32)

    @pl.loop(0, length // CONV_ROWS)
    def _(i):
        rows = chunk(i, CONV_ROWS)
        around = pl.ds(pl.multiple_of(i * CONV_ROWS, CONV_ROWS), CONV_ROWS + taps)
        d_area = dmix_ref[around, :]
        g_area = glu_ref[around, :]
        here = d_area[half : half + CONV_ROWS, :]
        total = jnp.zeros((CONV_ROWS, LANES), F32)
        for shift in range(8):
            d_moved = d_area[shift : shift + CONV_ROWS + taps - 8, :]
            g_moved = g_area[shift : shift + CONV_ROWS + taps - 8, :]
            for group in range(taps // 8):
                offset = 8 * group + shift
                part = slice(8 * group, 8 * group + CONV_ROWS)
                tap = taps - 1 - offset
                total += tap_ref[tap : tap + 1, :] * d_moved[part, :]
                if offset >= 1:
                    product = (here * g_moved[part, :]).reshape(CONV_ROWS // 8, 8, LANES)
                    acc_ref[offset - 1] += jnp.sum(product, axis=0)
        product = (here * g_area[taps : taps + CONV_ROWS, :]).reshape(CONV_ROWS // 8, 8, LANES)
        acc_ref[taps - 1] += jnp.sum(product, axis=0)
        grad_glu = total * valid_rows(i * CONV_ROWS, CONV_ROWS, valid)
        value = z_ref[rows, :LANES].astype(F32)
        sigma = sigmoid(z_ref[rows, LANES:].astype(F32))
        grad_value = (grad_glu * sigma).astype(BF)
        grad_gate = (grad_glu * value * sigma * (1.0 - sigma)).astype(BF)
        dz_ref[rows, :LANES] = grad_value
        dz_ref[rows, LANES:] = grad_gate
        unit_ref[0:1, :] += column_sum(grad_value.astype(F32))
        unit_ref[1:2, :] += column_sum(grad_gate.astype(F32))

    @pl.loop(0, count)
    def _(i):
        rows = chunk(i)
        out_ref[rows, :] += dot(dz_ref[rows, :], w_ref[:, : 2 * LANES], NT)

    grad_ref[:, : 2 * LANES] = dot(ht_ref[...], dz_ref[...]).astype(BF)
    grad_ref[:, 2 * LANES : 3 * LANES] = out_grad_ref[...]
    grad_taps = jnp.sum(acc_ref[...], axis=1)
    grad_ref[:, 3 * LANES :] = dot(
        tap_selector(taps, features, wide_count, True), grad_taps.astype(BF)
    ).astype(BF)

    @pl.when(step == pl.num_programs(0) - 1)
    def _():
        @pl.loop(0, count)
        def _(i):
            rows = chunk(i)
            grad_normed = out_ref[rows, :]
            normal, inverse_row = normal_rows(x_ref[rows, :])
            vec_ref[0:1, :] += column_sum(grad_normed * normal)
            vec_ref[1:2, :] += column_sum(grad_normed)
            result = up_ref[rows, :] + normal_rows_back(
                grad_normed, normal, inverse_row, gain_ref[2:3, :]
            )
            vec_ref[2:3, :] += column_sum(result)
            out_ref[rows, :] = result


def conv_backward(
    taps, wide_count, valid, upstream, x, h, gains, weights, z, mixed, dbn, stats, affine,
    out_grad, grads,
):
    length, features = x.shape
    blocks = weights.shape[0] // features
    column = pl.BlockSpec((length, LANES), lambda n: (0, n))

    def kernel(*refs):
        conv_backward_kernel(taps, wide_count, *refs[:12], *refs[13:])

    return pl.pallas_call(
        kernel,
        name="conv_backward",
        grid=(blocks,),
        in_specs=[
            pl.BlockSpec(memory_space=pltpu.SMEM),
            full(upstream.shape),
            full(x.shape),
            full(h.shape),
            full(gains.shape),
            pl.BlockSpec((features, 4 * LANES), lambda n: (n, 4)),
            pl.BlockSpec((length, 2 * LANES), lambda n: (0, n)),
            column,
            column,
            pl.BlockSpec((8, LANES), lambda n: (0, n)),
            pl.BlockSpec((2, LANES), lambda n: (0, n)),
            pl.BlockSpec((features, LANES), lambda n: (n, 0)),
            pl.BlockSpec(memory_space=pl.ANY),
        ],
        out_specs=[
            full((length, features)),
            pl.BlockSpec((features, 4 * LANES), lambda n: (n, 4)),
            pl.BlockSpec((8, LANES), lambda n: (0, n)),
            full((8, features)),
        ],
        out_shape=[
            jax.ShapeDtypeStruct((length, features), F32),
            jax.ShapeDtypeStruct(grads.shape, BF),
            jax.ShapeDtypeStruct((8, features), F32),
            jax.ShapeDtypeStruct((8, features), F32),
        ],
        scratch_shapes=[
            pltpu.VMEM((length + taps, LANES), F32),
            pltpu.VMEM((length + taps, LANES), F32),
            pltpu.VMEM((taps, LANES), F32),
            pltpu.VMEM((length, 2 * LANES), BF),
            pltpu.VMEM((features, length), BF),
            pltpu.VMEM((taps, 8, LANES), F32),
        ],
        input_output_aliases={12: 1},
        compiler_params=params(),
    )(valid, upstream, x, h, gains, weights, z, mixed, dbn, stats, affine, out_grad, grads)


def middle_kernel(
    len_ref, x2_ref, cot_ref, gain_ref, bias_ref, mixed_ref, stat_ref, affine_ref, wc_ref, wf_ref,
    hidden_ref,
    final_ref, dx3_ref, grad_ref, hidden_grad_ref, vec_ref, dbn_ref, sums_ref, out_grad_ref,
    x3_ref, dx4_ref, h_ref, ht_ref, df_ref, dft_ref, a_ref, s_ref, da_ref,
):
    phase = pl.program_id(0)
    step = pl.program_id(1)
    last = pl.num_programs(1) - 1
    length, features = x2_ref.shape
    count = length // ROWS
    width = hidden_ref.shape[1]
    valid = len_ref[0]
    mean = stat_ref[0:1, :]
    inverse_bn = stat_ref[1:2, :]

    @pl.when(phase == 0)
    def _():
        @pl.when(step == 0)
        def _():
            vec_ref[...] = jnp.zeros(vec_ref.shape, F32)

            @pl.loop(0, count)
            def _(i):
                rows = chunk(i)
                x3_ref[rows, :] = x2_ref[rows, :] + bias_ref[7:8, :]

        @pl.loop(0, count)
        def _(i):
            rows = chunk(i)
            normal = (mixed_ref[rows, :] - mean) * inverse_bn
            bn = normal * affine_ref[0:1, :] + affine_ref[1:2, :]
            act = (bn * sigmoid(bn)).astype(BF)
            x3_ref[rows, :] += dot(act, wc_ref[:, 2 * LANES : 3 * LANES], NT)

        @pl.when(step == last)
        def _():
            @pl.loop(0, count)
            def _(i):
                rows = chunk(i)
                normal, _ = normal_rows(x3_ref[rows, :])
                hidden = normal * gain_ref[3:4, :] + bias_ref[3:4, :]
                h_ref[rows, :] = hidden.astype(BF)
                ht_ref[:, rows] = hidden.T.astype(BF)
                dx4_ref[rows, :] = jnp.zeros((ROWS, features), F32)

    @pl.when(phase == 1)
    def _():
        @pl.loop(0, count)
        def _(i):
            rows = chunk(i)
            pre = dot(h_ref[rows, :], wf_ref[:, :width]) + hidden_ref[1:2, :]
            a_ref[step, rows, :] = pre
            act = (pre * sigmoid(pre)).astype(BF)
            dx4_ref[rows, :] += dot(act, wf_ref[:, width:], NT)

        @pl.when(step == last)
        def _():
            @pl.loop(0, count)
            def _(i):
                rows = chunk(i)
                x4 = x3_ref[rows, :] + 0.5 * (dx4_ref[rows, :] + bias_ref[8:9, :])
                normal, inverse = normal_rows(x4)
                final_ref[rows, :] = (normal * gain_ref[4:5, :] + bias_ref[4:5, :]).astype(BF)
                upstream = cot_ref[rows, :].astype(F32) * valid_rows(i * ROWS, ROWS, valid)
                vec_ref[0:1, :] += column_sum(upstream * normal)
                vec_ref[1:2, :] += column_sum(upstream)
                dx4 = normal_rows_back(upstream, normal, inverse, gain_ref[4:5, :])
                dx4_ref[rows, :] = dx4
                half = 0.5 * dx4
                vec_ref[2:3, :] += column_sum(half)
                df_ref[rows, :] = half.astype(BF)
                dft_ref[:, rows] = half.T.astype(BF)
                dx3_ref[rows, :] = jnp.zeros((ROWS, features), F32)

    @pl.when(phase == 2)
    def _():
        hidden_grad_ref[...] = jnp.zeros(hidden_grad_ref.shape, F32)

        @pl.loop(0, count)
        def _(i):
            rows = chunk(i)
            pre = a_ref[step, rows, :]
            sigma = sigmoid(pre)
            s_ref[rows, :] = (pre * sigma).astype(BF)
            grad_act = dot(df_ref[rows, :], wf_ref[:, width:])
            grad_pre = (grad_act * (sigma * (1.0 + pre * (1.0 - sigma)))).astype(BF)
            da_ref[rows, :] = grad_pre
            hidden_grad_ref[...] += column_sum(grad_pre.astype(F32))
            dx3_ref[rows, :] += dot(grad_pre, wf_ref[:, :width], NT)

        @pl.loop(0, features // LANES)
        def _(i):
            rows = chunk(i, LANES)
            grad_ref[rows, :width] = dot(ht_ref[rows, :], da_ref[...]).astype(BF)
            grad_ref[rows, width:] = dot(dft_ref[rows, :], s_ref[...]).astype(BF)

        @pl.when(step == last)
        def _():
            @pl.loop(0, count)
            def _(i):
                rows = chunk(i)
                grad_normed = dx3_ref[rows, :]
                normal, inverse = normal_rows(x3_ref[rows, :])
                vec_ref[3:4, :] += column_sum(grad_normed * normal)
                vec_ref[4:5, :] += column_sum(grad_normed)
                result = dx4_ref[rows, :] + normal_rows_back(
                    grad_normed, normal, inverse, gain_ref[3:4, :]
                )
                vec_ref[5:6, :] += column_sum(result)
                dx3_ref[rows, :] = result
                df_ref[rows, :] = result.astype(BF)
                dft_ref[:, rows] = result.T.astype(BF)

    @pl.when(phase == 3)
    def _():
        sums_ref[...] = jnp.zeros(sums_ref.shape, F32)

        @pl.loop(0, count)
        def _(i):
            rows = chunk(i)
            normal = (mixed_ref[rows, :] - mean) * inverse_bn
            bn = normal * affine_ref[0:1, :] + affine_ref[1:2, :]
            sigma = sigmoid(bn)
            s_ref[rows, :LANES] = (bn * sigma).astype(BF)
            grad_act = dot(df_ref[rows, :], wc_ref[:, 2 * LANES : 3 * LANES])
            grad_bn = grad_act * (sigma * (1.0 + bn * (1.0 - sigma)))
            dbn_ref[rows, :] = grad_bn
            sums_ref[0:1, :] += column_sum(grad_bn)
            sums_ref[1:2, :] += column_sum(grad_bn * normal)

        out_grad_ref[...] = dot(dft_ref[...], s_ref[:, :LANES]).astype(BF)


def middle(valid, x2, cotangent, gains, biases, mixed, stats, affine, weights, hidden):
    length, features = x2.shape
    blocks = weights.shape[0] // features
    width = hidden.shape[1] // blocks
    final = blocks - 1

    def outer(phase, n):
        return jnp.where((phase == 0) | (phase == 3), n, final)

    def late(phase, n):
        return jnp.where(phase == 3, n, 0)

    def inner(phase, n):
        return jnp.where(phase == 0, 0, jnp.where(phase == 3, final, n))

    def backs(phase, n):
        return jnp.where(phase < 2, 0, jnp.where(phase == 3, final, n))

    return pl.pallas_call(
        middle_kernel,
        name="middle",
        grid=(4, blocks),
        in_specs=[
            pl.BlockSpec(memory_space=pltpu.SMEM),
            full(x2.shape),
            full(cotangent.shape),
            full(gains.shape),
            full(biases.shape),
            pl.BlockSpec((length, LANES), lambda p, n: (0, outer(p, n))),
            pl.BlockSpec((8, LANES), lambda p, n: (0, outer(p, n))),
            pl.BlockSpec((2, LANES), lambda p, n: (0, outer(p, n))),
            pl.BlockSpec((features, 4 * LANES), lambda p, n: (outer(p, n), 4)),
            pl.BlockSpec((features, 2 * width), lambda p, n: (inner(p, n), 1)),
            pl.BlockSpec((2, width), lambda p, n: (0, inner(p, n))),
        ],
        out_specs=[
            full((length, features)),
            full((length, features)),
            pl.BlockSpec((features, 2 * width), lambda p, n: (backs(p, n), 1)),
            pl.BlockSpec((1, width), lambda p, n: (0, backs(p, n))),
            full((8, features)),
            pl.BlockSpec((length, LANES), lambda p, n: (0, late(p, n))),
            pl.BlockSpec((8, LANES), lambda p, n: (0, late(p, n))),
            pl.BlockSpec((features, LANES), lambda p, n: (late(p, n), 0)),
        ],
        out_shape=[
            jax.ShapeDtypeStruct((length, features), BF),
            jax.ShapeDtypeStruct((length, features), F32),
            jax.ShapeDtypeStruct(weights.shape, BF),
            jax.ShapeDtypeStruct((1, blocks * width), F32),
            jax.ShapeDtypeStruct((8, features), F32),
            jax.ShapeDtypeStruct((length, features), F32),
            jax.ShapeDtypeStruct((8, features), F32),
            jax.ShapeDtypeStruct((blocks * features, LANES), BF),
        ],
        scratch_shapes=[
            pltpu.VMEM((length, features), F32),
            pltpu.VMEM((length, features), F32),
            pltpu.VMEM((length, features), BF),
            pltpu.VMEM((features, length), BF),
            pltpu.VMEM((length, features), BF),
            pltpu.VMEM((features, length), BF),
            pltpu.VMEM((blocks, length, width), F32),
            pltpu.VMEM((length, width), BF),
            pltpu.VMEM((length, width), BF),
        ],
        compiler_params=params(),
    )(valid, x2, cotangent, gains, biases, mixed, stats, affine, weights, weights, hidden)


def position_table(length, feature_count):
    step = 32
    column = np.arange(feature_count)
    frequency = np.exp((column // 2) * (-2.0 * math.log(10000.0) / feature_count))
    phase = (column % 2) * (math.pi / 2)
    high = (length - 1 - step * np.arange(2 * length // step))[:, None] * frequency[None, :]
    low = -np.arange(step)[:, None] * frequency[None, :] + phase[None, :]
    high_sin, high_cos, low_sin, low_cos = (
        jnp.asarray(part.astype(np.float32))
        for part in (np.sin(high), np.cos(high), np.sin(low), np.cos(low))
    )
    table = high_sin[:, None, :] * low_cos[None] + high_cos[:, None, :] * low_sin[None]
    return table.reshape(2 * length, feature_count).astype(BF)


def shards(
    mesh_shape,
    inputs,
    cotangent,
    lengths,
    ffn1_in,
    ffn1_out,
    attn_in,
    pos_proj,
    attn_out,
    conv_in,
    depthwise,
    conv_out,
    ffn2_in,
    ffn2_out,
    row_gains,
    row_biases,
    unit_biases,
    ffn_biases,
    norm_affine,
):
    narrow, wide = mesh_shape["narrow"], mesh_shape["wide"]
    both = ("narrow", "wide")
    micros, frames, utters, features = inputs.shape
    streams = micros * utters
    copies = narrow // streams
    assert copies * streams == narrow
    length = frames * narrow
    blocks = features // LANES
    depth = features // wide
    each = attn_out.shape[0]
    hidden_each = ffn_biases.shape[1]
    taps_each = depthwise.shape[0]
    taps = taps_each * wide
    narrow_index = lax.axis_index("narrow")
    stream_index = narrow_index // copies

    smalls = jnp.concatenate(
        [unit_biases, norm_affine, ffn_biases.reshape(-1, each)], axis=0
    )
    extra = jnp.concatenate([depthwise, smalls], axis=0)
    extra = jnp.pad(extra, ((0, depth - extra.shape[0]), (0, 0)))
    packed = jnp.concatenate(
        [
            ffn1_in,
            ffn1_out.T,
            ffn2_in,
            ffn2_out.T,
            conv_in.reshape(depth, -1),
            conv_out.T,
            extra,
            attn_in.reshape(depth, -1),
            pos_proj,
            attn_out.T,
        ],
        axis=1,
    )
    kinds = (
        (1, hidden_each), (1, hidden_each), (1, hidden_each), (1, hidden_each),
        (2, each), (1, each), (1, each), (3, each), (1, each), (1, each),
    )
    gathered = lax.all_gather(packed, both, axis=0, tiled=True)

    def pieces(array, parts_of):
        begin = 0
        for many, size in parts_of:
            yield array[..., begin : begin + many * size], many, size
            begin += many * size

    small_rows = gathered.reshape(narrow, features, -1)[
        :, taps_each : taps_each + SMALL_ROWS, 4 * hidden_each + 3 * each : 4 * hidden_each + 4 * each
    ].astype(F32)
    units = jnp.moveaxis(small_rows[:, :5], 0, 1).reshape(5, features)
    affine = jnp.moveaxis(small_rows[:, 5:7], 0, 1).reshape(2, features)
    hidden_biases = jnp.moveaxis(
        small_rows[:, 7:].reshape(narrow, 2, hidden_each), 0, 1
    ).reshape(2, -1)
    if narrow != blocks:
        regrouped = []
        for part, many, size in pieces(gathered.reshape(narrow, features, -1), kinds):
            part = part.reshape(narrow, features, many, size)
            part = part.transpose(1, 2, 0, 3).reshape(features, many, blocks, -1)
            regrouped.append(part.transpose(2, 0, 1, 3).reshape(blocks * features, -1))
        gathered = jnp.concatenate(regrouped, axis=1)

    gains = row_gains.astype(F32)
    biases = row_biases.astype(F32)
    table = position_table(length, features)

    def to_stream(array):
        moved = array.transpose(0, 2, 1, 3).reshape(streams, frames, features)
        if copies > 1:
            moved = jnp.repeat(moved, copies, axis=0)
        moved = lax.all_to_all(moved, "narrow", 0, 0, tiled=True)
        return moved.reshape(length, features)

    def from_stream(array):
        moved = lax.all_to_all(
            array.reshape(narrow, frames, features), "narrow", 0, 0, tiled=True
        )[::copies]
        return moved.reshape(micros, utters, frames, features).transpose(0, 2, 1, 3)

    x0 = to_stream(inputs)
    upstream = to_stream(cotangent)
    valid = lax.dynamic_slice(lengths.reshape(-1), (stream_index,), (1,))
    masked = jnp.where(jnp.arange(length)[None, :] < valid, 0.0, MASKED).astype(F32)

    hops = [("narrow", copies << bit) for bit in range(utters.bit_length() - 1)]
    hops += [("wide", 1 << bit) for bit in range(wide.bit_length() - 1)]

    def swap(array, axis, mask):
        size = mesh_shape[axis]
        return lax.ppermute(array, axis, [(i, i ^ mask) for i in range(size)])

    def merge_moments(local_stats, local_valid):
        size = jnp.broadcast_to(local_valid.astype(F32), (1, features))
        state = jnp.concatenate([local_stats[:2], size], axis=0)
        for axis, mask in hops:
            other = swap(state, axis, mask)
            total = state[2:] + other[2:]
            delta = other[:1] - state[:1]
            share = other[2:] / total
            state = jnp.concatenate(
                [
                    state[:1] + delta * share,
                    state[1:2] + other[1:2] + delta * delta * state[2:] * share,
                    total,
                ],
                axis=0,
            )
        return state

    def merge_sums(state):
        for axis, mask in hops:
            state = state + swap(state, axis, mask)
        return state

    x1, a_first = ffn_forward(x0, gains, biases, gathered, hidden_biases)
    x2, *saved = attention_forward(x1, gains, biases, gathered, units, table, masked)
    h3, z, mixed, local_stats = conv_forward(
        taps, wide, valid, x2, gains, biases, gathered, units
    )
    moments = merge_moments(local_stats, valid)
    number = moments[2:]
    stats = jnp.concatenate([moments[:1], lax.rsqrt(moments[1:2] / number + EPSILON)], axis=0)
    stats = jnp.pad(stats, ((0, 6), (0, 0)))

    final, dx3, grads, hidden_second, vec_mid, dbn, local_sums, out_grad = middle(
        valid, x2, upstream, gains, biases, mixed, stats, affine, gathered, hidden_biases
    )
    sums = merge_sums(local_sums[:2])
    stats = jnp.concatenate([stats[:2], sums / number, jnp.zeros((4, features), F32)], axis=0)
    dx2, grads, unit_conv, vec_conv = conv_backward(
        taps, wide, valid, dx3, x2, h3, gains, gathered, z, mixed, dbn, stats, affine,
        out_grad, grads,
    )
    dx1, grads, unit_att, vec_att = attention_backward(
        dx2, x1, saved, gains, gathered, table, grads
    )
    dx0, grads, hidden_first, vec_first = ffn_backward(
        dx1, x0, gains, biases, gathered, a_first, grads
    )

    layer_out = from_stream(final)
    input_grad = from_stream(dx0.astype(BF)).astype(F32)

    vectors = jnp.concatenate(
        [
            vec_first[0:1], vec_att[0:1], vec_conv[0:1], vec_mid[3:4], vec_mid[0:1],
            vec_first[1:2], vec_att[1:2], vec_conv[1:2], vec_mid[4:5], vec_mid[1:2],
            vec_first[2:3], vec_conv[2:3], vec_mid[5:6], vec_mid[2:3],
            unit_att[:3], unit_conv[:2],
            local_sums[1:2], local_sums[0:1],
            hidden_first.reshape(-1, features), hidden_second.reshape(-1, features),
        ],
        axis=0,
    )
    vectors = lax.psum(vectors, both) * (1.0 / copies)
    grad_gains = vectors[:5]
    grad_biases = vectors[5:14]

    def own_columns(array, size):
        return lax.dynamic_slice_in_dim(array, narrow_index * size, size, 1)

    grad_units = own_columns(vectors[14:19], each)
    grad_affine = own_columns(vectors[19:21], each)
    grad_hidden = own_columns(vectors[21:].reshape(2, -1), hidden_each)

    if narrow != blocks:
        ratio = narrow // blocks
        regrouped = []
        block_kinds = tuple((many, size * ratio) for many, size in kinds)
        for part, many, size in pieces(grads.reshape(blocks, features, -1), block_kinds):
            part = part.reshape(blocks, features, many, ratio, size // ratio)
            part = part.transpose(0, 3, 1, 2, 4)
            regrouped.append(part.reshape(narrow * features, -1))
        grads = jnp.concatenate(regrouped, axis=1)
    reduced = lax.psum_scatter(grads, both, scatter_dimension=0, tiled=True)
    if copies > 1:
        reduced = reduced * (1.0 / copies)
    outs = [part.astype(F32) for part, _, _ in pieces(reduced, kinds)]
    return (
        layer_out,
        input_grad,
        outs[0],
        outs[1].T,
        outs[7].reshape(depth, 3, each),
        outs[8],
        outs[9].T,
        outs[4].reshape(depth, 2, each),
        outs[6][:taps_each],
        outs[5].T,
        outs[2],
        outs[3].T,
        grad_gains,
        grad_biases,
        grad_units,
        grad_hidden,
        grad_affine,
    )


def solution(mesh):
    shape = dict(mesh.shape)
    matrix_in = P("wide", "narrow")
    matrix_out = P("narrow", "wide")
    stacked = P("wide", None, "narrow")
    stream = P(None, "narrow", "wide", None)
    weights = (
        matrix_in, matrix_out, stacked, matrix_in, matrix_out,
        stacked, matrix_in, matrix_out, matrix_in, matrix_out,
    )
    vectors = (P(), P(), P(None, "narrow"), P(None, "narrow"), P(None, "narrow"))
    return jax.shard_map(
        partial(shards, shape),
        mesh=mesh,
        in_specs=(stream, stream, P(None, "wide")) + weights + vectors,
        out_specs=(stream, stream) + weights + vectors,
        check_vma=False,
    )
```

time: 2640 us -> 727 us (0.28)
  waiting for transfers between devices: 1120 us -> 317 us
  local copies, waits for them, and re-layouts: 530 us -> 30.3 us
  blocking collectives: 448 us -> 56.4 us
  matrix products: 298 us -> 0 us
  Pallas kernels: 0 us -> 263 us
  other arithmetic: 210 us -> 19.8 us
    reduce_scatter x25 -> x1, waiting for transfers between devices: 995 us -> 195 us  [shards(): reduced = lax.psum_scatter(grads, both, scatter_dimension=0, tiled=True)]
    all_gather x10 -> x0, blocking collectives: 309 us -> none  [the longest x1 33.6 us: fetch_weights(): lax.all_gather(ffn2_in, 'wide', axis=0, tiled=True)]
    dot_general x87 -> x0, matrix products: 298 us -> none  [the longest x4 27.1 us: block_scores(): jnp.einsum('qd,wd->qw', rows_p, window, preferred_element_type=jnp.float32)]
    reshape x16 -> x10, local copies, waits for them, and re-layouts: 287 us -> 2.69 us  [the longest x1 0.69 us: shards(): ffn_biases.reshape(-1, each)]
    pallas_call x0 -> x7, Pallas kernels: none -> 263 us  [the longest x1 65.1 us: attention_backward(): pl.pallas_call(kernel, name='attention_backward', grid=(blocks,), in_spec...]
    reduce_sum x47 -> x0, other arithmetic: 89.4 us -> none  [the longest x4 17.1 us: conv_backward(): jnp.sum(grad_mixed * padded[tap_index:tap_index + length], axis=(0, 1))]
    slice x21 -> x12, local copies, waits for them, and re-layouts: 80.7 us -> 5.97 us  [the longest x1 0.83 us: shards(): vec_first[2:3]]
    pad x8 -> x0, local copies, waits for them, and re-layouts: 60.5 us -> none  [the longest x4 42.9 us: unshift_rows(): flattened = jnp.pad(padded.reshape(-1), (block_rows - 1, 1))]
  transfers between devices with their start and end apart: 41 -> 14, of which waited for: 28 -> 11; matrix products, arithmetic and copies ran while one was open for 28% -> 4% of each run, Pallas kernels for 0% -> 0%
where the time goes in v1:
time: 727 us; the launch traced here: 725 us
  waiting for transfers between devices  317 us (44%)
  Pallas kernels  263 us (36%)
  blocking collectives  56.4 us (8%)
  local copies, waits for them, and re-layouts  30.3 us (4%)
  starting transfers between devices  23.4 us (3%)
  other arithmetic  19.8 us (3%)
  between operations  15.1 us (2%)
    reduce_scatter x1, waiting for transfers between devices, shards(): reduced = lax.psum_scatter(grads, both, scatter_dimension=0, tiled=True)  195 us
    all_gather x1, waiting for transfers between devices, shards(): gathered = lax.all_gather(packed, both, axis=0, tiled=True)  90.2 us
    pallas_call x1, Pallas kernels, attention_backward(): pl.pallas_call(kernel, name='attention_backward', grid=(blocks,), in_spec...  65.1 us
    psum x1, blocking collectives, shards(): vectors = lax.psum(vectors, both) * (1.0 / copies)  56.4 us
    pallas_call x1, Pallas kernels, attention_forward(): pl.pallas_call(attention_forward_kernel, name='attention_forward', grid=(...  53 us
    pallas_call x1, Pallas kernels, middle(): pl.pallas_call(middle_kernel, name='middle', grid=(4, blocks), in_specs=[...  50 us
    pallas_call x1, Pallas kernels, conv_backward(): pl.pallas_call(kernel, name='conv_backward', grid=(blocks,), in_specs=[pl...  34.4 us
    pallas_call x1, Pallas kernels, ffn_backward(): pl.pallas_call(kernel, name='ffn_backward', grid=(blocks,), in_specs=[ful...  25.4 us
  transfers between devices with their start and end apart: 14, of which 11 were waited for; matrix products, arithmetic and copies ran while one was open for 4% of the time, Pallas kernels for 0%

profile of v1, /device:TPU:0, one launch (start us, length us, event | category | flops | bytes accessed | tf_op | source)
XLA Modules:
  0.0 724.9 jit_solution(10625263553470652533)
XLA Ops:
  7.3 0.8 constant_dynamic-update-slice_fusion.5
  8.8 0.8 bitcast_dynamic-update-slice_fusion.1
  9.6 0.8 constant_dynamic-update-slice_fusion.4
  10.5 0.8 bitcast_dynamic-update-slice_fusion
  15.9 2.4 copy.45
  18.3 4.2 all-to-all-start
  23.2 1.2 compare_select_fusion.masked_ref
  26.4 2.0 add_convert_fusion
  28.4 90.2 %all-gather.2.cloned.1.call-done.w_ref.wc_ref.wf_ref.refs_5_.refs_4_.w = bf16[2048,3200]{1,0:T(8,128)(2,1)} async-done(((bf16[64,3200]{1,0:T(8,128)(2,1)}), bf16[2048,3200]{1,0:T(8,128)(2,1)}) %all-gather.2.cloned.1.call-update) | async-done | bytes 13107216 | tf_op jit(solution)/shard_map/all_gather | solution.py:1054
  120.6 1.0 copy-done.2
  121.6 14.0 %ffn_forward.1 = (f32[1024,512]{1,0:T(8,128)}, bf16[1024,2048]{1,0:T(8,128)(2,1)}) custom-call(bf16[1024,512]{1,0:T(8,128)(2,1)} %bitcast.67, f32[5,512]{1,0:T(8,128)} %convert_element_type.51.gain_ref.refs_4_.refs_3_.g, f32[9,512]{1,0:T(8,128)} %convert_element_type.52.bias_ref.b, ...), custom_call_target="tpu_custom_call" | custom-call | tf_op jit(solution)/shard_map/ffn_forward/pallas_call | solution.py:102
  135.6 53.0 %attention_forward.1 = (f32[1024,512]{1,0:T(8,128)}, bf16[1024,512]{1,0:T(8,128)(2,1)}, bf16[1024,512]{1,0:T(8,128)(2,1)}, bf16[1024,512]{1,0:T(8,128)(2,1)}, bf...) custom-call(f32[1024,512]{1,0:T(8,128)} %get-tuple-element.52.x_ref., ...), custom_call_target="tpu_custom_call" | custom-call | tf_op jit(solution)/shard_map/attention_forward/pallas_call | solution.py:297
  188.7 21.4 %conv_forward.1 = (bf16[1024,512]{1,0:T(8,128)(2,1)}, bf16[1024,1024]{1,0:T(8,128)(2,1)}, f32[1024,512]{1,0:T(8,128)}, f32[8,512]{1,0:T(8,128)}) custom-call(s32[1]{0:T(128)} %dynamic_slice.12.len_ref.refs_0_, f32[1024,512]{1,0:T(8,128)} %get-tuple-element.53.x_ref.x2_ref.refs_2_, f32[5,512]{1,0:T(8,128)} %convert_element_type.51.gain_ref.refs_4_.refs_3_.g, ...), custom_call_target="tpu_custom_call" | custom-call | tf_op jit(solution)/shard_map/conv_forward/pallas_call | solution.py:578
  211.2 0.9 collective-permute-done
  213.6 1.5 collective-permute-start.1
  215.2 2.2 collective-permute-done.1
  217.4 1.2 collective-permute-start.2
  218.6 1.2 copy.48
  219.8 3.5 all-to-all-start.1
  223.6 1.3 collective-permute-start.3
  225.6 2.7 collective-permute-done.3
  228.9 8.8 %all-to-all-done.1 = bf16[4,256,512]{2,1,0:T(8,128)(2,1)S(1)} async-done(((bf16[4,256,512]{2,1,0:T(8,128)(2,1)}), bf16[4,256,512]{2,1,0:T(8,128)(2,1)S(1)}, u32[]{:S(2)}, u32[]{:S(2)}) %all-to-all-start.1) | async-done | bytes 1048608 | tf_op jit(solution)/shard_map/all_to_all | solution.py:1086
  237.7 1.0 copy-done.3
  238.7 50.0 %middle.1 = (bf16[1024,512]{1,0:T(8,128)(2,1)}, f32[1024,512]{1,0:T(8,128)}, bf16[2048,3200]{1,0:T(8,128)(2,1)}, f32[1,2048]{1,0:T(1,128)}, f32[8,512]{1,0:T(8,1...) custom-call(s32[1]{0:T(128)} %dynamic_slice.12.len_ref.refs_0_, ...), custom_call_target="tpu_custom_call" | custom-call | tf_op jit(solution)/shard_map/middle/pallas_call | solution.py:926
  289.5 1.2 collective-permute-done.4
  291.4 1.5 collective-permute-start.5
  292.8 2.1 collective-permute-done.5
  295.0 0.9 collective-permute-start.6
  295.8 2.7 collective-permute-done.6
  298.6 1.3 collective-permute-start.7
  299.9 3.2 collective-permute-done.7
  303.8 34.4 %conv_backward.1 = (f32[1024,512]{1,0:T(8,128)}, bf16[2048,3200]{1,0:T(8,128)(2,1)}, f32[8,512]{1,0:T(8,128)}, f32[8,512]{1,0:T(8,128)}) custom-call(s32[1]{0:T(128)} %dynamic_slice.12.len_ref.refs_0_, f32[1024,512]{1,0:T(8,128)} %get-tuple-element.57.refs_1_, f32[1024,512]{1,0:T(8,128)} %get-tuple-element.53.x_ref.x2_ref.refs_2_, ...), custom_call_target="tpu_custom_call", output_to_operand_aliasing={{1}: (12, {})} | custom-call | tf_op jit(solution)/shard_map/conv_backward/pallas_call | solution.py:730
  338.2 65.1 %attention_backward.1 = (f32[1024,512]{1,0:T(8,128)}, bf16[2048,3200]{1,0:T(8,128)(2,1)}, f32[8,512]{1,0:T(8,128)}, f32[8,512]{1,0:T(8,128)}) custom-call(f32[1024,512]{1,0:T(8,128)} %get-tuple-element.64.refs_0_, f32[1024,512]{1,0:T(8,128)} %get-tuple-element.52.x_ref.refs_1_, ...), custom_call_target="tpu_custom_call", output_to_operand_aliasing={{1}: (13, {})} | custom-call | tf_op jit(solution)/shard_map/attention_backward/pallas_call | solution.py:453
  403.3 25.4 %ffn_backward.1 = (f32[1024,512]{1,0:T(8,128)}, bf16[2048,3200]{1,0:T(8,128)(2,1)}, f32[1,2048]{1,0:T(1,128)}, f32[8,512]{1,0:T(8,128)}) custom-call(f32[1024,512]{1,0:T(8,128)} %get-tuple-element.74.up, bf16[1024,512]{1,0:T(8,128)(2,1)} %bitcast.68, f32[5,512]{1,0:T(8,128)} %convert_element_type.51.gain_ref.refs_4_.refs_3_.g, ...), custom_call_target="tpu_custom_call", output_to_operand_aliasing={{1}: (6, {})} | custom-call | tf_op jit(solution)/shard_map/ffn_backward/pallas_call | solution.py:194
  428.7 3.9 all-to-all-start.2
  436.1 1.1 convert_element_type.58
  437.2 0.8 fusion.19
  438.0 0.8 fusion.18
  438.9 7.9 %all-to-all-done.2 = bf16[4,256,512]{2,1,0:T(8,128)(2,1)S(1)} async-done(((bf16[4,256,512]{2,1,0:T(8,128)(2,1)}), bf16[4,256,512]{2,1,0:T(8,128)(2,1)S(1)}, u32[]{:S(2)}, u32[]{:S(2)}) %all-to-all-start.2) | async-done | bytes 1048608 | tf_op jit(solution)/shard_map/all_to_all | solution.py:1090
  446.8 3.5 all-to-all-start.3
  451.4 56.4 %psum.7 = f32[29,512]{1,0:T(8,128)S(1)} all-reduce(f32[29,512]{1,0:T(8,128)S(1)} %concatenate.36), channel_id=1, replica_groups=mesh['wide'=8,'narrow'=4] {'narrow','wide'}, use_global_device_ids=true, to_apply=%region_1.2 | all-reduce | flops 14848 | bytes 118784 | tf_op jit(solution)/shard_map/psum | solution.py:1170
  510.8 2.0 copy.49
  513.2 2.9 copy.50
  516.1 194.7 %reduce-scatter.2.cloned.1.call-done = bf16[64,3200]{1,0:T(8,128)(2,1)} async-done(((bf16[2048,3200]{1,0:T(8,128)(2,1)}), bf16[64,3200]{1,0:T(8,128)(2,1)}) %reduce-scatter.2.cloned.1.call-update) | async-done | bytes 409616 | tf_op jit(solution)/shard_map/reduce_scatter | solution.py:1190
  712.2 1.7 convert_bitcast_fusion.1
  713.9 1.4 convert_bitcast_fusion.4
  715.3 1.4 copy_bitcast_fusion
  716.8 1.3 slice_convert_fusion.5
  (105 shorter events, 24.8 us)
Async XLA Ops:
  7.2 6.4 copy-start
  7.2 111.4 %all-gather.2.cloned.1.call-start = ((), (), s32[]{:S(2)}) async-start(), calls=%async_computation.5 | async-start | bytes 13516800 | tf_op jit(solution)/shard_map/all_gather | solution.py:1054
  15.0 0.8 copy-start.6
  15.8 6.8 copy-start.18
  15.8 9.3 %copy-start.13 = (bf16[5,512]{1,0:T(8,128)(2,1)S(1)}, bf16[5,512]{1,0:T(8,128)(2,1)}, u32[]{:S(2)}) copy-start(bf16[5,512]{1,0:T(8,128)(2,1)} %param.35) | copy-start | bytes 15364
  15.8 9.9 %copy-start.11 = (bf16[9,512]{1,0:T(8,128)(2,1)S(1)}, bf16[9,512]{1,0:T(8,128)(2,1)}, u32[]{:S(2)}) copy-start(bf16[9,512]{1,0:T(8,128)(2,1)} %param.36) | copy-start | bytes 27652
  15.8 10.5 %copy-start.7 = (f32[64,512]{1,0:T(8,128)S(1)}, f32[64,512]{1,0:T(8,128)}, u32[]{:S(2)}) copy-start(f32[64,512]{1,0:T(8,128)} %constant.45.clone) | copy-start | bytes 393220
  15.8 10.5 %copy-start.8 = (f32[64,512]{1,0:T(8,128)S(1)}, f32[64,512]{1,0:T(8,128)}, u32[]{:S(2)}) copy-start(f32[64,512]{1,0:T(8,128)} %constant.46.clone) | copy-start | bytes 393220
  15.9 10.5 %copy-start.9 = (f32[32,512]{1,0:T(8,128)S(1)}, f32[32,512]{1,0:T(8,128)}, u32[]{:S(2)}) copy-start(f32[32,512]{1,0:T(8,128)} %constant.47.clone) | copy-start | bytes 196612
  15.9 10.5 %copy-start.10 = (f32[32,512]{1,0:T(8,128)S(1)}, f32[32,512]{1,0:T(8,128)}, u32[]{:S(2)}) copy-start(f32[32,512]{1,0:T(8,128)} %constant.48.clone) | copy-start | bytes 196612
  18.3 102.3 %all-to-all-start = ((bf16[4,256,512]{2,1,0:T(8,128)(2,1)}), bf16[4,256,512]{2,1,0:T(8,128)(2,1)S(1)}, u32[]{:S(2)}, u32[]{:S(2)}) async-start(bf16[4,256,512]{2,1,0:T(8,128)(2,1)} %bitcast.1), calls=%async_computation | async-start | bytes 2097152 | tf_op jit(solution)/shard_map/all_to_all | solution.py:1086
  120.6 1.0 copy-start.2
  188.6 21.5 %copy-start.17 = (pred[3]{0:T(512)(128)(4,1)S(1)}, pred[3]{0:T(512)(128)(4,1)}, u32[]{:S(2)}) copy-start(pred[3]{0:T(512)(128)(4,1)} %constant.40.clone.1) | copy-start | bytes 13
  188.7 30.0 %copy-start.5 = (bf16[2,256,2,512]{3,2,1,0:T(2,128)(2,1)S(1)}, bf16[2,256,2,512]{3,2,1,0:T(2,128)(2,1)}, u32[]{:S(2)}) copy-start(bf16[2,256,2,512]{3,2,1,0:T(2,128)(2,1)} %param.23) | copy-start | bytes 3145732
  210.9 1.2 collective-permute-start
  213.6 3.7 collective-permute-start.1
  217.4 6.2 collective-permute-start.2
  219.8 17.9 %all-to-all-start.1 = ((bf16[4,256,512]{2,1,0:T(8,128)(2,1)}), bf16[4,256,512]{2,1,0:T(8,128)(2,1)S(1)}, u32[]{:S(2)}, u32[]{:S(2)}) async-start(bf16[4,256,512]{2,1,0:T(8,128)(2,1)} %bitcast.14), calls=%async_computation.1 | async-start | bytes 2097152 | tf_op jit(solution)/shard_map/all_to_all | solution.py:1086
  223.3 487.4 %reduce-scatter.2.cloned.1.call-start = ((), (), s32[]{:S(2)}) async-start(), calls=%async_computation.6 | async-start | bytes 13516800 | tf_op jit(solution)/shard_map/reduce_scatter | solution.py:1190
  223.6 4.6 collective-permute-start.3
  237.7 1.0 copy-start.3
  289.5 1.2 collective-permute-start.4
  291.4 3.6 collective-permute-start.5
  295.0 3.6 collective-permute-start.6
  298.6 4.5 collective-permute-start.7
  428.7 4.5 copy-start.14
  428.7 5.1 copy-start.12
  428.7 6.0 copy-start.15
  428.7 6.6 copy-start.16
  428.7 7.4 %copy-start.4 = (f32[1024,512]{1,0:T(8,128)S(1)}, f32[1024,512]{1,0:T(8,128)}, u32[]{:S(2)}) copy-start(f32[1024,512]{1,0:T(8,128)} %get-tuple-element.77) | copy-start | bytes 6291460
  428.7 18.1 %all-to-all-start.2 = ((bf16[4,256,512]{2,1,0:T(8,128)(2,1)}), bf16[4,256,512]{2,1,0:T(8,128)(2,1)S(1)}, u32[]{:S(2)}, u32[]{:S(2)}) async-start(bf16[4,256,512]{2,1,0:T(8,128)(2,1)} %bitcast.72), calls=%async_computation.2 | async-start | bytes 2097152 | tf_op jit(solution)/shard_map/all_to_all | solution.py:1090
  446.8 66.1 %all-to-all-start.3 = ((bf16[4,256,512]{2,1,0:T(8,128)(2,1)}), bf16[4,256,512]{2,1,0:T(8,128)(2,1)S(1)}, u32[]{:S(2)}, u32[]{:S(2)}) async-start(bf16[4,256,512]{2,1,0:T(8,128)(2,1)} %bitcast.25), calls=%async_computation.3 | async-start | bytes 2097152 | tf_op jit(solution)/shard_map/all_to_all | solution.py:1090
  512.9 205.2 %copy-start.1 = (bf16[64,3,128]{2,0,1:T(8,128)(2,1)S(1)}, bf16[64,3,128]{2,0,1:T(8,128)(2,1)}, u32[]{:S(2)}) copy-start(bf16[64,3,128]{2,0,1:T(8,128)(2,1)} %param.27) | copy-start | bytes 147460
Sparse Core Ops, SparseCore 0:
  15.9 102.6 all-gather.1
  428.8 281.9 reduce-scatter.1
